TPU v7x, 256 devices: a whole 4x4x8 slice. The times are simulated.
256 devices in a mesh: dir: 32 (over z, y_hi, core), freq: 8 (over x, y_lo).
Axes of the slice: x: 4, y: 4 (y_hi: 2, y_lo: 2; y = y_hi * 2 + y_lo), z: 8, core: 2. Of those that a mesh axis runs over, the one named last changes fastest.
Arguments:
- spectrum: float32 [64, 48, 8192], P('dir', 'freq'), may hold values from 0.1 to 1
- neighbours: int32 [6, 8192], replicated, may hold values from 0 to 8191
- edge_angle: float32 [6, 8192], replicated, may hold values from -3.140625 to 3.140625
- edge_coef: float32 [6, 8192], replicated, may hold values from 0.02 to 0.1
- land_mask: int32 [8192], replicated, may hold values 0 or 1
- dia_offsets: int32 [2, 3], replicated, may hold values from 1 to 6, as said below
- dia_coef: float32 [3], replicated, may hold values from 0.2 to 1
- space_order: int32 [8192], replicated, may hold values from 0 to 8191, each once
- wind_speed: float32 [8192], P(('dir', 'freq')), may hold values from 0.5 to 2.5
- wind_dir: float32 [8192], P(('dir', 'freq')), may hold values from -3.140625 to 3.140625
Outputs:
- new_spectrum: float32 [64, 48, 8192], P(None, None, ('dir', 'freq'))
Inputs may be any that keep to these rules, and one draw needn't show every extreme that they name: `dia_offsets`: row 0 holds direction offsets from 1 to 6, one of them 6; row 1 holds frequency offsets from 1 to 2, one of them 2.
All inputs are finite; a program needn't handle non-finite values.
Results may differ from a plain program's by a relative error of at most 0.00061.
Values may be sent and summed in bfloat16 or wider, within the bound.
No kernel may reach another device: no remote copies, remote signals or barrier semaphores. Data moves between devices by JAX's collectives and lax.ppermute only.
A program may use at most 64 MiB of HBM per device.

v0:
```python
import math

import jax
import jax.numpy as jnp
from jax import lax
from jax.sharding import PartitionSpec as P

NFREQ = 48
DSPAN = 6
FSPAN = 2


SIG_LO = 0.35
SIG_HI = 2.8
DT_NL = 0.1
CDS = 0.05
APM = 0.4
BETA = 0.05
INV_FLOOR = 0.01


def padded(cells, sides, width):
    for axis, dim in sides:
        count = lax.axis_size(axis)
        ends = count - 1
        head = lax.slice_in_dim(cells, 0, width, axis=dim)
        tail = lax.slice_in_dim(cells, cells.shape[dim] - width, cells.shape[dim], axis=dim)
        cells = jnp.concatenate(
            [
                lax.ppermute(tail, axis, [(i, (i + 1) % count) for i in range(ends)]),
                cells,
                lax.ppermute(head, axis, [((i + 1) % count, i) for i in range(ends)]),
            ],
            axis=dim,
        )
    return cells


def from_behind(array, axis, by):
    count = lax.axis_size(axis)
    return lax.ppermute(array, axis, [(i, (i + by) % count) for i in range(count)])


def frequencies(first, count, total):
    index = (first + jnp.arange(count, dtype=jnp.int32)).astype(jnp.float32)
    return SIG_LO * jnp.exp(index * (math.log(SIG_HI / SIG_LO) / (total - 1)))


def reorder_points(field, order):
    return jnp.take(field, order, axis=2)


def propagate(field, neighbours, edge_angle, edge_coef, wetness, theta, speed):
    masked = field * wetness[None, None, :]
    total = field
    for k in range(neighbours.shape[0]):
        beside = jnp.take(masked, neighbours[k], axis=2)
        geometry = edge_coef[k][None, :] * jnp.maximum(
            jnp.cos(theta[:, None] - edge_angle[k][None, :]), 0.0
        )
        total = total + speed[None, :, None] * geometry[:, None, :] * (beside - field)
    return total


def nonlinear(window, center, dpad, offsets, dia_coef):
    ndirs, nfreqs, npoints = center.shape
    total = jnp.zeros(center.shape, jnp.float32)
    for q in range(dia_coef.shape[0]):
        dshift = offsets[0, q]
        fshift = offsets[1, q]
        zero_start = jnp.zeros((), jnp.int32)
        upper = lax.dynamic_slice(
            window, (dpad + dshift, FSPAN + fshift, zero_start), (ndirs, nfreqs, npoints)
        ).astype(jnp.float32)
        lower = lax.dynamic_slice(
            window, (dpad - dshift, FSPAN - fshift, zero_start), (ndirs, nfreqs, npoints)
        ).astype(jnp.float32)
        delta = center * center * (upper + lower) - 2.0 * center * upper * lower
        total = total + dia_coef[q] * delta
    return total


def on_device(
    spectrum,
    neighbours,
    edge_angle,
    edge_coef,
    land_mask,
    dia_offsets,
    dia_coef,
    space_order,
    wind_speed,
    wind_dir,
):
    dir_dev, freq_dev, npoints = spectrum.shape
    ndirs = dir_dev * lax.axis_size("dir")
    first_dir = lax.axis_index("dir") * dir_dev
    first_freq = lax.axis_index("freq") * freq_dev
    theta = (
        2.0
        * math.pi
        / ndirs
        * (first_dir + jnp.arange(dir_dev, dtype=jnp.int32)).astype(jnp.float32)
    )
    speed = 0.5 / frequencies(first_freq, freq_dev, NFREQ)
    wetness = land_mask.astype(jnp.float32)
    old = spectrum.astype(jnp.bfloat16)
    moved = propagate(spectrum, neighbours, edge_angle, edge_coef, wetness, theta, speed)
    rimmed = padded(old, (("freq", 1),), FSPAN)
    reach = DSPAN // dir_dev
    lower_blocks = [from_behind(rimmed, "dir", step) for step in range(reach, 0, -1)]
    upper_blocks = [from_behind(rimmed, "dir", -step) for step in range(1, reach + 1)]
    window = jnp.concatenate(lower_blocks + [rimmed] + upper_blocks, axis=0)
    transfer = nonlinear(window, old.astype(jnp.float32), DSPAN, dia_offsets, dia_coef)
    payload = wetness[None, None, :] * (moved + DT_NL * transfer)
    relaid = lax.all_to_all(
        lax.all_to_all(
            reorder_points(payload, space_order), "dir", split_axis=2, concat_axis=0, tiled=True
        ),
        "freq",
        split_axis=2,
        concat_axis=1,
        tiled=True,
    )
    sigma = frequencies(0, NFREQ, NFREQ)
    theta_all = 2.0 * math.pi / ndirs * jnp.arange(ndirs, dtype=jnp.int32).astype(jnp.float32)
    weight = 1.0 / (relaid.shape[0] * relaid.shape[1])
    etot = jnp.sum(relaid, axis=(0, 1)) * weight
    inverse = jnp.sum(relaid / sigma[None, :, None], axis=(0, 1)) * weight
    msig = jnp.clip(etot / jnp.maximum(inverse, INV_FLOOR), SIG_LO, SIG_HI)
    steep = etot * msig**4 / APM
    rate = (
        CDS
        * (sigma[None, :, None] / msig[None, None, :]) ** 2
        * msig[None, None, :]
        * steep[None, None, :] ** 2
    )
    alignment = jnp.cos(theta_all[:, None] - wind_dir[None, :])
    growth = (
        BETA
        * sigma[None, :, None]
        * jnp.maximum(
            wind_speed[None, None, :] * sigma[None, :, None] * alignment[:, None, :] - 1.0, 0.0
        )
    )
    return relaid * (1.0 + growth) / (1.0 + rate)


def solution(mesh):
    in_specs = (
        P("dir", "freq", None),
        P(),
        P(),
        P(),
        P(),
        P(),
        P(),
        P(),
        P(("dir", "freq")),
        P(("dir", "freq")),
    )
    out_specs = P(None, None, ("dir", "freq"))
    return jax.shard_map(
        on_device, mesh=mesh, in_specs=in_specs, out_specs=out_specs, check_vma=False
    )
```

profile of v0, /device:TPU:1, one launch (start us, length us, event | category | flops | bytes accessed | tf_op | source)
XLA Modules:
  0.0 707.9 jit_solution(5620367257727269005)
XLA Ops:
  0.8 1.4 fusion.40
  2.4 1.3 collective-permute-start.1
  3.7 4.7 collective-permute-start
  8.4 2.1 fusion.43
  11.2 1.4 fusion.32
  13.4 2.2 fusion.42
  15.6 2.0 fusion.41
  17.6 6.1 maximum_multiply_fusion.5
  23.7 1.6 fusion.45
  40.1 7.9 %copy.178 = f32[2,6,8192]{1,0,2:T(2,128)} copy(f32[2,6,8192]{2,0,1:T(2,128)S(1)} %get-tuple-element.9) | data formatting | bytes 786432 | tf_op jit(solution)/shard_map/mul | solution.py:54
  48.0 59.7 %gather_fusion.5 = f32[8192,2,6]{2,1,0:T(2,128)} fusion(f32[2,6,8192]{1,0,2:T(2,128)} %copy.178, s32[8192]{0:T(1024)S(1)} %fusion.31), kind=kCustom, calls=%fused_computation.5.clone | custom fusion | bytes 819200 | tf_op jit(solution)/shard_map/jit(_take)/gather | solution.py:57
  107.7 9.3 %copy.189 = f32[8192,2,6]{0,1,2:T(2,128)S(1)} copy(f32[8192,2,6]{2,1,0:T(2,128)} %gather_fusion.5) | data formatting | bytes 786432 | tf_op jit(solution)/shard_map/jit(_take)/gather | solution.py:57
  117.1 59.7 %gather_fusion.4 = f32[8192,2,6]{2,1,0:T(2,128)} fusion(f32[2,6,8192]{1,0,2:T(2,128)} %copy.178, s32[8192]{0:T(1024)S(1)} %fusion.30), kind=kCustom, calls=%fused_computation.4.clone | custom fusion | bytes 819200 | tf_op jit(solution)/shard_map/jit(_take)/gather | solution.py:57
  176.7 10.1 %copy.187 = f32[8192,2,6]{0,1,2:T(2,128)} copy(f32[8192,2,6]{2,1,0:T(2,128)} %gather_fusion.4) | data formatting | bytes 786432 | tf_op jit(solution)/shard_map/jit(_take)/gather | solution.py:57
  186.8 59.7 %gather_fusion.3 = f32[8192,2,6]{2,1,0:T(2,128)} fusion(f32[2,6,8192]{1,0,2:T(2,128)} %copy.178, s32[8192]{0:T(1024)S(1)} %fusion.29), kind=kCustom, calls=%fused_computation.3.clone | custom fusion | bytes 819200 | tf_op jit(solution)/shard_map/jit(_take)/gather | solution.py:57
  246.5 10.1 %copy.185 = f32[8192,2,6]{0,1,2:T(2,128)} copy(f32[8192,2,6]{2,1,0:T(2,128)} %gather_fusion.3) | data formatting | bytes 786432 | tf_op jit(solution)/shard_map/jit(_take)/gather | solution.py:57
  256.6 59.7 %gather_fusion.2 = f32[8192,2,6]{2,1,0:T(2,128)} fusion(f32[2,6,8192]{1,0,2:T(2,128)} %copy.178, s32[8192]{0:T(1024)S(1)} %fusion.28), kind=kCustom, calls=%fused_computation.2.clone | custom fusion | bytes 819200 | tf_op jit(solution)/shard_map/jit(_take)/gather | solution.py:57
  316.3 10.1 %copy.183 = f32[8192,2,6]{0,1,2:T(2,128)} copy(f32[8192,2,6]{2,1,0:T(2,128)} %gather_fusion.2) | data formatting | bytes 786432 | tf_op jit(solution)/shard_map/jit(_take)/gather | solution.py:57
  326.4 59.7 %gather_fusion.1 = f32[8192,2,6]{2,1,0:T(2,128)} fusion(f32[2,6,8192]{1,0,2:T(2,128)} %copy.178, s32[8192]{0:T(1024)S(1)} %fusion.27), kind=kCustom, calls=%fused_computation.1.clone | custom fusion | bytes 819200 | tf_op jit(solution)/shard_map/jit(_take)/gather | solution.py:57
  386.1 10.1 %copy.181 = f32[8192,2,6]{0,1,2:T(2,128)} copy(f32[8192,2,6]{2,1,0:T(2,128)} %gather_fusion.1) | data formatting | bytes 786432 | tf_op jit(solution)/shard_map/jit(_take)/gather | solution.py:57
  396.1 59.7 %gather_fusion = f32[8192,2,6]{2,1,0:T(2,128)} fusion(f32[2,6,8192]{1,0,2:T(2,128)} %copy.178, s32[8192]{0:T(1024)S(1)} %fusion.26), kind=kCustom, calls=%fused_computation.clone | custom fusion | bytes 819200 | tf_op jit(solution)/shard_map/jit(_take)/gather | solution.py:57
  455.8 10.1 %copy.179 = f32[8192,2,6]{0,1,2:T(2,128)} copy(f32[8192,2,6]{2,1,0:T(2,128)} %gather_fusion) | data formatting | bytes 786432 | tf_op jit(solution)/shard_map/jit(_take)/gather | solution.py:57
  466.5 3.0 collective-permute-start.2
  470.8 2.9 collective-permute-start.3
  473.7 2.1 collective-permute-start.4
  475.9 2.2 collective-permute-start.6
  478.1 6.4 collective-permute-done.2
  484.5 1.5 collective-permute-start.7
  487.2 8.2 %collective-permute-done.3 = bf16[2,10,8192]{2,0,1:T(2,128)(2,1)S(1)} collective-permute-done((bf16[2,10,8192]{2,0,1:T(2,128)(2,1)S(1)}, bf16[2,10,8192]{2,0,1:T(2,128)(2,1)S(1)}, u32[]{:S(2)}, u32[]{:S(2)}) %collective-permute-start.3) | collective-permute-done | bytes 327712 | tf_op jit(solution)/shard_map/ppermute | solution.py:41
  495.4 3.5 collective-permute-done.4
  498.9 1.5 collective-permute-done.5
  501.8 10.0 %concatenate.7 = bf16[14,10,8192]{2,0,1:T(8,128)(2,1)S(1)} concatenate(bf16[2,10,8192]{2,0,1:T(2,128)(2,1)} %copy-done, bf16[2,10,8192]{2,0,1:T(2,128)(2,1)} %copy-done.1, bf16[2,10,8192]{2,0,1:T(2,128)(2,1)} %copy-done.2, bf16[2,10,8192]{2,0,1:T(2,128)(2,1)S(1)} %pad_maximum_fusion, bf16[2,10,8192]{2,0,1:T(2,128)(2,1)} %copy-done.3, bf16[2,10,8192]{2,0,1:T(2,128)(2,1)} %copy-done.4, ...), dimensions={0} | concatenate | bytes 4587520 | tf_op jit(solution)/shard_map/concatenate | solution.py:113
  511.9 8.8 %fusion.15 = f32[2,6,8192]{2,0,1:T(2,128)} fusion(f32[2,6,8192]{2,0,1:T(2,128)} %param.12, f32[8192,2,6]{0,1,2:T(2,128)S(1)} %copy.189, f32[8192,2,6]{0,1,2:T(2,128)} %copy.187, f32[8192,2,6]{0,1,2:T(2,128)} %copy.185, f32[8192,2,6]{0,1,2:T(2,128)} %copy.183, f32[8192,2,6]{0,1,2:T(2,128)} %copy.181, f32[8192,2,6]{0,1,2:T(2,128)} %copy.179, ...), kind=kLoop, calls=%fused_computation.37 | loop fusion | flops 6094848 | bytes 4997204 | tf_op jit(solution)/shard_map/mul | solution.py:115
  520.7 9.3 %copy.194 = f32[2,6,8192]{1,0,2:T(2,128)} copy(f32[2,6,8192]{2,0,1:T(2,128)} %fusion.15) | data formatting | bytes 786432 | tf_op jit(solution)/shard_map/mul | solution.py:115
  530.0 59.7 %gather_fusion.6 = f32[8192,2,6]{2,1,0:T(2,128)} fusion(f32[2,6,8192]{1,0,2:T(2,128)} %copy.194, s32[8192]{0:T(1024)S(1)} %copy-done.6), kind=kCustom, calls=%fused_computation.6.clone | custom fusion | bytes 819200 | tf_op jit(solution)/shard_map/jit(_take)/gather | solution.py:50
  589.6 30.8 %fusion.47 = f32[8192,2,6]{2,1,0:T(2,128)} fusion(f32[8192,2,6]{2,1,0:T(2,128)} %gather_fusion.6, pred[8192]{0:T(1024)(128)(4,1)S(1)} %compare_and_fusion), kind=kLoop, calls=%fused_computation.106 | loop fusion | flops 98304 | bytes 794624
  620.5 15.0 %reshape.535 = f32[32,1,3072]{2,1,0:T(1,128)} reshape(f32[8192,2,6]{2,1,0:T(2,128)} %fusion.47) | data formatting | bytes 786432
  635.5 12.1 %all-to-all-start = ((f32[32,1,3072]{2,1,0:T(1,128)}), f32[32,1,3072]{2,1,0:T(1,128)S(1)}, u32[]{:S(2)}, u32[]{:S(2)}) async-start(f32[32,1,3072]{2,1,0:T(1,128)} %reshape.535), calls=%async_computation | async-start | bytes 786432 | tf_op jit(solution)/shard_map/all_to_all | solution.py:117
  647.6 14.4 %all-to-all-done = f32[32,1,3072]{2,1,0:T(1,128)S(1)} async-done(((f32[32,1,3072]{2,1,0:T(1,128)}), f32[32,1,3072]{2,1,0:T(1,128)S(1)}, u32[]{:S(2)}, u32[]{:S(2)}) %all-to-all-start) | async-done | bytes 393248 | tf_op jit(solution)/shard_map/all_to_all | solution.py:117
  662.6 1.5 reduce.5
  664.1 14.4 %reshape.536 = f32[8192,2,6]{2,1,0:T(2,128)} reshape(f32[32,3072]{1,0:T(8,128)S(1)} %reduce.5) | data formatting | bytes 786432
  678.6 9.9 %copy.195 = f32[2,6,32,256]{3,0,2,1:T(2,128)S(1)} copy(f32[2,6,32,256]{1,0,3,2:T(2,128)} %bitcast.117) | data formatting | bytes 786432 | tf_op jit(solution)/shard_map/all_to_all | solution.py:117
  689.2 1.3 reshape.537
  690.5 5.9 all-to-all-start.1
  696.5 6.2 all-to-all-done.1
  702.7 1.5 reduce.6
  704.6 1.0 bitcast_reduce_fusion
  706.5 1.4 fusion
  (62 shorter events, 9.6 us)
Async XLA Ops:
  0.8 116.3 %copy-start.5 = (f32[8192]{0:T(1024)}, f32[8192]{0:T(1024)S(1)}, u32[]{:S(2)}) copy-start(f32[8192]{0:T(1024)S(1)} %convert_element_type.64) | copy-start | bytes 98308
  2.4 463.5 %collective-permute-start.1 = (bf16[2,2,8192]{2,1,0:T(2,128)(2,1)S(1)}, bf16[2,2,8192]{2,1,0:T(2,128)(2,1)S(1)}, u32[]{:S(2)}, u32[]{:S(2)}) collective-permute-start(bf16[2,2,8192]{2,1,0:T(2,128)(2,1)S(1)} %copy.191), channel_id=1, source_target_pairs={{1,0},{2,1},{3,2},{4,3},{5,4},{6,5},{7,6},{9,8},{10,9},{11,10},{12... | collective-permute-start | bytes 196616 | tf_op jit(solution)/shard_map/ppermute | solution.py:32
  3.7 462.2 %collective-permute-start = (bf16[2,2,8192]{2,1,0:T(2,128)(2,1)S(1)}, bf16[2,2,8192]{2,1,0:T(2,128)(2,1)S(1)}, u32[]{:S(2)}, u32[]{:S(2)}) collective-permute-start(bf16[2,2,8192]{2,1,0:T(2,128)(2,1)S(1)} %copy.190), channel_id=1, source_target_pairs={{0,1},{1,2},{2,3},{3,4},{4,5},{5,6},{6,7},{8,9},{9,10},{10,11},{11... | collective-permute-start | bytes 196616 | tf_op jit(solution)/shard_map/ppermute | solution.py:30
  386.1 83.5 %copy-start.7 = (f32[3]{0:T(128)S(1)}, f32[3]{0:T(128)}, u32[]{:S(2)}) copy-start(f32[3]{0:T(128)} %param.18) | copy-start | bytes 40
  466.5 18.0 %collective-permute-start.2 = (bf16[2,10,8192]{2,0,1:T(2,128)(2,1)S(1)}, bf16[2,10,8192]{2,0,1:T(2,128)(2,1)S(1)}, u32[]{:S(2)}, u32[]{:S(2)}) collective-permute-start(bf16[2,10,8192]{2,0,1:T(2,128)(2,1)S(1)} %pad_maximum_fusion), channel_id=1, source_target_pairs={{0,24},{8,32},{16,40},{24,48},{32,56},{40,64},{48,72},{56,80},{64,... | collective-permute-start | bytes 983048 | tf_op jit(solution)/shard_map/ppermute | solution.py:41
  470.8 24.6 %collective-permute-start.3 = (bf16[2,10,8192]{2,0,1:T(2,128)(2,1)S(1)}, bf16[2,10,8192]{2,0,1:T(2,128)(2,1)S(1)}, u32[]{:S(2)}, u32[]{:S(2)}) collective-permute-start(bf16[2,10,8192]{2,0,1:T(2,128)(2,1)S(1)} %pad_maximum_fusion), channel_id=1, source_target_pairs={{0,16},{8,24},{16,32},{24,40},{32,48},{40,56},{48,64},{56,72},{64,... | collective-permute-start | bytes 983048 | tf_op jit(solution)/shard_map/ppermute | solution.py:41
  473.7 25.1 %collective-permute-start.4 = (bf16[2,10,8192]{2,0,1:T(2,128)(2,1)S(1)}, bf16[2,10,8192]{2,0,1:T(2,128)(2,1)S(1)}, u32[]{:S(2)}, u32[]{:S(2)}) collective-permute-start(bf16[2,10,8192]{2,0,1:T(2,128)(2,1)S(1)} %pad_maximum_fusion), channel_id=1, source_target_pairs={{0,8},{8,16},{16,24},{24,32},{32,40},{40,48},{48,56},{56,64},{64,7... | collective-permute-start | bytes 983048 | tf_op jit(solution)/shard_map/ppermute | solution.py:41
  475.9 24.5 %collective-permute-start.5 = (bf16[2,10,8192]{2,0,1:T(2,128)(2,1)S(1)}, bf16[2,10,8192]{2,0,1:T(2,128)(2,1)S(1)}, u32[]{:S(2)}, u32[]{:S(2)}) collective-permute-start(bf16[2,10,8192]{2,0,1:T(2,128)(2,1)S(1)} %pad_maximum_fusion), channel_id=1, source_target_pairs={{0,248},{8,0},{16,8},{24,16},{32,24},{40,32},{48,40},{56,48},{64,5... | collective-permute-start | bytes 983048 | tf_op jit(solution)/shard_map/ppermute | solution.py:41
  475.9 24.5 %collective-permute-start.6 = (bf16[2,10,8192]{2,0,1:T(2,128)(2,1)S(1)}, bf16[2,10,8192]{2,0,1:T(2,128)(2,1)S(1)}, u32[]{:S(2)}, u32[]{:S(2)}) collective-permute-start(bf16[2,10,8192]{2,0,1:T(2,128)(2,1)S(1)} %pad_maximum_fusion), channel_id=1, source_target_pairs={{0,240},{8,248},{16,0},{24,8},{32,16},{40,24},{48,32},{56,40},{64,... | collective-permute-start | bytes 983048 | tf_op jit(solution)/shard_map/ppermute | solution.py:41
  484.5 15.8 %copy-start = (bf16[2,10,8192]{2,0,1:T(2,128)(2,1)}, bf16[2,10,8192]{2,0,1:T(2,128)(2,1)S(1)}, u32[]{:S(2)}) copy-start(bf16[2,10,8192]{2,0,1:T(2,128)(2,1)S(1)} %collective-permute-done.2) | copy-start | bytes 983044
  484.5 17.3 %collective-permute-start.7 = (bf16[2,10,8192]{2,0,1:T(2,128)(2,1)S(1)}, bf16[2,10,8192]{2,0,1:T(2,128)(2,1)}, u32[]{:S(2)}, u32[]{:S(2)}) collective-permute-start(bf16[2,10,8192]{2,0,1:T(2,128)(2,1)S(1)} %pad_maximum_fusion), channel_id=1, source_target_pairs={{0,232},{8,240},{16,248},{24,0},{32,8},{40,16},{48,24},{56,32},{64... | collective-permute-start | bytes 983048 | tf_op jit(solution)/shard_map/ppermute | solution.py:41
  495.4 5.0 copy-start.1
  498.9 1.5 copy-start.2
  500.3 0.8 copy-start.3
  501.1 0.7 copy-start.4
  511.9 18.1 %copy-start.6 = (s32[8192]{0:T(1024)S(1)}, s32[8192]{0:T(1024)}, u32[]{:S(2)}) copy-start(s32[8192]{0:T(1024)} %fusion.32) | copy-start | bytes 98308
  635.5 26.5 %all-to-all-start = ((f32[32,1,3072]{2,1,0:T(1,128)}), f32[32,1,3072]{2,1,0:T(1,128)S(1)}, u32[]{:S(2)}, u32[]{:S(2)}) async-start(f32[32,1,3072]{2,1,0:T(1,128)} %reshape.535), calls=%async_computation | async-start | bytes 786432 | tf_op jit(solution)/shard_map/all_to_all | solution.py:117
  678.6 17.7 %copy-start.9 = (f32[32]{0:T(128)S(1)}, f32[32]{0:T(128)}, u32[]{:S(2)}) copy-start(f32[32]{0:T(128)} %param.21) | copy-start | bytes 388
  678.6 27.8 %copy-start.8 = (f32[32]{0:T(128)S(1)}, f32[32]{0:T(128)}, u32[]{:S(2)}) copy-start(f32[32]{0:T(128)} %param.20) | copy-start | bytes 388
  690.5 12.2 %all-to-all-start.1 = ((f32[8,1,12288]{2,1,0:T(1,128)}), f32[8,1,12288]{2,1,0:T(1,128)S(1)}, u32[]{:S(2)}, u32[]{:S(2)}) async-start(f32[8,1,12288]{2,1,0:T(1,128)} %reshape.537), calls=%async_computation.1 | async-start | bytes 786432 | tf_op jit(solution)/shard_map/all_to_all | solution.py:116
where the time goes:
time: 714 us; the launch traced here: 708 us
  local copies, waits for them, and re-layouts  558 us (78%)
  other arithmetic  59.1 us (8%)
  waiting for transfers between devices  40.2 us (6%)
  starting transfers between devices  35.6 us (5%)
  between operations  15.2 us (2%)
    gather x12, local copies, waits for them, and re-layouts, propagate(): beside = jnp.take(masked, neighbours[k], axis=2)  418 us
    gather x1, local copies, waits for them, and re-layouts, reorder_points(): return jnp.take(field, order, axis=2)  59.7 us
    unnamed x24, local copies, waits for them, and re-layouts  32.6 us
    unnamed x1, other arithmetic  30.8 us
    ppermute x6, waiting for transfers between devices, from_behind(): lax.ppermute(array, axis, [(i, (i + by) % count) for i in range(count)])  19.6 us
    all_to_all x1, waiting for transfers between devices, on_device(): lax.all_to_all(reorder_points(payload, space_order), 'dir', split_axis=2,...  14.4 us
  transfers between devices with their start and end apart: 10, of which 6 were waited for; matrix products, arithmetic and copies ran while one was open for 63% of the time, Pallas kernels for 0%

commit v1 on v0

v1 whole, which is shorter than its diff:
```python
import functools
import math

import jax
import jax.numpy as jnp
from jax import lax
from jax.experimental import pallas as pl
from jax.experimental.pallas import tpu as pltpu
from jax.sharding import PartitionSpec as P

NFREQ = 48
DSPAN = 6
FSPAN = 2

SIG_LO = 0.35
SIG_HI = 2.8
DT_NL = 0.1
CDS = 0.05
APM = 0.4
BETA = 0.05
INV_FLOOR = 0.01

LANES = 128
TILE = 256
CENTRE = 0.5


def sigma_of(index):
    return SIG_LO * jnp.exp(index.astype(jnp.float32) * (math.log(SIG_HI / SIG_LO) / (NFREQ - 1)))


def one_hot(low, ramp):
    return jnp.where(ramp == low.astype(jnp.float32).astype(jnp.bfloat16), 1.0, 0.0).astype(jnp.bfloat16)


def local_kernel(
    ndirs, spec_at, nbr_at, angle_at, coef_at, mask_at, order_at, out,
    spec, nbr, angle, coef, mask, order, arrived, field, pickf, pick, geom, wet, keepf, keep, ramp
):
    dirs, freqs, npoints = 2, spec.shape[0], spec.shape[2]
    pairs = [(spec_at, spec), (mask_at, mask), (angle_at, angle)]
    pairs += [(coef_at, coef), (nbr_at, nbr), (order_at, order)]
    copies = [
        pltpu.make_async_copy(src, dst, arrived.at[n]) for n, (src, dst) in enumerate(pairs)
    ]
    for copy in copies:
        copy.start()
    tiles = npoints // TILE
    first_dir = lax.axis_index("dir") * dirs
    first_freq = lax.axis_index("freq") * freqs
    sub = lax.broadcasted_iota(jnp.int32, (8, TILE), 0)
    lane = lax.broadcasted_iota(jnp.int32, (8, LANES), 1)
    speed = 0.5 / sigma_of(first_freq + sub)
    ramp[...] = lax.broadcasted_iota(jnp.int32, (TILE, TILE), 0).astype(jnp.float32).astype(jnp.bfloat16)
    pad = jnp.zeros((8 - freqs, TILE), jnp.float32)

    for copy in copies[:4]:
        copy.wait()

    def stage(t, carry):
        at = pl.ds(pl.multiple_of(t * TILE, TILE), TILE)
        wet_row = mask[:, at].astype(jnp.float32)
        wet[:, at] = wet_row
        for i in range(dirs):
            rows = [spec[f, pl.ds(i, 1), at] for f in range(freqs)]
            value = jnp.concatenate(rows + [pad], axis=0)
            field[i, :, at] = value
            shown = value * wet_row - CENTRE
            spot = pl.ds(i * freqs * tiles + t, freqs, stride=tiles)
            for c in range(TILE // LANES):
                pickf[c, spot, :] = shown[:freqs, c * LANES : (c + 1) * LANES]
            theta = (2.0 * math.pi / ndirs) * (first_dir + i).astype(jnp.float32)
            bearing = jnp.cos(theta - angle[:, at])
            geom[i, :, at] = coef[:, at] * jnp.maximum(bearing, 0.0)
        return carry

    lax.fori_loop(0, tiles, stage, 0)
    for c in range(TILE // LANES):
        pick[:, c * LANES : (c + 1) * LANES] = pickf[c].astype(jnp.bfloat16)

    groups = tiles // 8

    copies[4].wait()

    def advect(t, carry):
        at = pl.ds(pl.multiple_of(t * TILE, TILE), TILE)
        total = [jnp.zeros((8, TILE), jnp.float32) for _ in range(dirs * freqs)]
        weight = [jnp.zeros((1, TILE), jnp.float32) for _ in range(dirs)]
        for k in range(nbr.shape[0]):
            index = nbr[k : k + 1, at]
            low = jnp.bitwise_and(index, TILE - 1)
            high = jnp.broadcast_to(jnp.right_shift(index, 8), (8, TILE))
            found = jnp.dot(pick[...], one_hot(low, ramp[...]), preferred_element_type=jnp.float32)
            match = [high == sub + 8 * h for h in range(groups)]
            for i in range(dirs):
                row = geom[i, k : k + 1, at]
                weight[i] = weight[i] + row
                for f in range(freqs):
                    r = i * freqs + f
                    chosen = jnp.zeros((8, TILE), jnp.float32)
                    for h in range(groups):
                        start = r * tiles + 8 * h
                        chosen = jnp.where(match[h], found[start : start + 8], chosen)
                    total[r] = total[r] + row * chosen
        wet_row = wet[:, at]
        kept, rest = [], []
        for i in range(dirs):
            value = field[i, :, at]
            rows = [
                jnp.sum(total[i * freqs + f], axis=0, keepdims=True) for f in range(freqs)
            ]
            inflow = jnp.concatenate(rows + [pad], axis=0)
            moved = value + speed * (inflow + weight[i] * (CENTRE - value))
            old = value.astype(jnp.bfloat16).astype(jnp.float32)
            kept.append(wet_row * old)
            rest.append(wet_row * (moved - old))
        for g, part in enumerate(kept + rest):
            keepf[pl.ds(pl.multiple_of(t * 32, 32) + 8 * g, 8), :] = part
        return carry

    lax.fori_loop(0, tiles, advect, 0, unroll=4)
    keep[...] = keepf[...].astype(jnp.bfloat16)

    copies[5].wait()

    def swap(t, carry):
        at = pl.ds(pl.multiple_of(t * TILE, TILE), TILE)
        index = order[:, at]
        low = jnp.bitwise_and(index, TILE - 1)
        high = jnp.broadcast_to(jnp.right_shift(index, 8), (8, TILE))
        found = jnp.dot(keep[...], one_hot(low, ramp[...]), preferred_element_type=jnp.float32)
        part = [jnp.zeros((8, TILE), jnp.float32) for _ in range(4)]
        for h in range(tiles):
            match = high == h
            for g in range(4):
                start = 32 * h + 8 * g
                part[g] = jnp.where(match, found[start : start + 8], part[g])
        for c in range(TILE // LANES):
            v = [x[:, c * LANES : (c + 1) * LANES] for x in part]
            left = lane < 64
            w0 = jnp.where(left, v[0], pltpu.roll(v[2], 64, 1))
            w2 = jnp.where(left, pltpu.roll(v[0], 64, 1), v[2])
            w1 = jnp.where(left, v[1], pltpu.roll(v[3], 64, 1))
            w3 = jnp.where(left, pltpu.roll(v[1], 64, 1), v[3])
            even = jnp.bitwise_and(lane, 32) == 0
            blocks = [
                jnp.where(even, w0, pltpu.roll(w1, 32, 1)),
                jnp.where(even, pltpu.roll(w0, 96, 1), w1),
                jnp.where(even, w2, pltpu.roll(w3, 32, 1)),
                jnp.where(even, pltpu.roll(w2, 96, 1), w3),
            ]
            for b in range(4):
                out[t * 8 + c * 4 + b] = blocks[b].astype(jnp.bfloat16)
        return carry

    lax.fori_loop(0, tiles, swap, 0, unroll=4)


def finish_kernel(
    freq_blocks, offsets, strength, wind_speed, wind_dir, blocks, out, table, relaid, rows
):
    nblocks, _, _ = blocks.shape
    pairs = nblocks // freq_blocks
    reach = DSPAN // 2
    freqs = NFREQ // freq_blocks
    low_pad = 8
    lane = lax.broadcasted_iota(jnp.int32, (NFREQ, LANES), 1)
    first = lane < 32
    half = lane < 64
    ndirs = 2 * pairs
    npts = 32

    edge = jnp.zeros((8, LANES), jnp.float32)
    for parity in range(2):
        for s in range(pairs + 2 * reach):
            table[parity, s, 0:8] = edge
            table[parity, s, low_pad + NFREQ : low_pad + NFREQ + 8] = edge

    def unpack(s, carry):
        for b in range(freq_blocks):
            piece = blocks[s * freq_blocks + b].astype(jnp.float32)
            table[0, s + reach, low_pad + b * freqs : low_pad + (b + 1) * freqs] = piece[:freqs]
        body = table[0, s + reach, low_pad : low_pad + NFREQ]
        turned = jnp.where(first, pltpu.roll(body, LANES - 32, 1), pltpu.roll(body, 32, 1))
        table[1, s + reach, low_pad : low_pad + NFREQ] = turned
        return carry

    lax.fori_loop(0, pairs, unpack, 0)
    for parity in range(2):
        for s in range(reach):
            table[parity, s] = table[parity, s + pairs]
            table[parity, s + pairs + reach] = table[parity, s + reach]

    def transfer(s, carry):
        total = carry
        body = table[0, s + reach, low_pad : low_pad + NFREQ]
        moved = body + pltpu.roll(body, 64, 1)
        change = jnp.zeros((NFREQ, LANES), jnp.float32)
        for q in range(strength.shape[0]):
            d = offsets[0, q]
            m = offsets[1, q]
            odd = jnp.bitwise_and(d, 1)

            def shifted(by, start):
                near = s + reach + jnp.right_shift(by, 1)
                far = s + reach + jnp.right_shift(by + 1, 1)
                at = pl.ds(low_pad + start, NFREQ)
                return jnp.where(first, table[odd, near, at], table[odd, far, at])

            upper = shifted(d, m)
            lower = shifted(-d, -m)
            delta = body * body * (upper + lower) - 2.0 * body * upper * lower
            change = change + strength[q] * delta
        value = moved + DT_NL * change
        relaid[s] = value
        return total + value

    total = lax.fori_loop(0, pairs, transfer, jnp.zeros((NFREQ, LANES), jnp.float32))

    sigma = sigma_of(lax.broadcasted_iota(jnp.int32, (NFREQ, LANES), 0))
    weight = 1.0 / (ndirs * NFREQ)

    def over_dirs(x):
        x = jnp.sum(x, axis=0, keepdims=True)
        x = jnp.broadcast_to(x, (8, LANES))
        lane8 = lane[:8]
        x = x + jnp.where(lane8 < 32, pltpu.roll(x, LANES - 32, 1), pltpu.roll(x, 32, 1))
        return x[:1]

    etot = over_dirs(total) * weight
    inverse = over_dirs(total / sigma) * weight
    msig = jnp.clip(etot / jnp.maximum(inverse, INV_FLOOR), SIG_LO, SIG_HI)
    steep = etot * (msig * msig * msig * msig) / APM
    ratio = sigma / msig
    rate = CDS * (ratio * ratio) * msig * (steep * steep)
    damp = 1.0 / (1.0 + rate)
    wind = jnp.concatenate([wind_speed[...]] * 4, axis=1) * sigma
    towards = jnp.concatenate([wind_dir[...]] * 4, axis=1)
    step = lax.broadcasted_iota(jnp.int32, (pairs, LANES), 0) * 2 + jnp.bitwise_and(
        jnp.right_shift(lax.broadcasted_iota(jnp.int32, (pairs, LANES), 1), 5), 1
    )
    rows[...] = jnp.cos((2.0 * math.pi / ndirs) * step.astype(jnp.float32) - towards)
    push = BETA * sigma

    def grow(s, carry):
        growth = push * jnp.maximum(wind * rows[pl.ds(s, 1), :] - 1.0, 0.0)
        value = relaid[s] * (1.0 + growth) * damp
        out[s] = value[:, :64]
        return carry

    lax.fori_loop(0, pairs, grow, 0)


def local_call(
    ndirs, parts, spectrum, neighbours, edge_angle, edge_coef, land_mask, space_order
):
    dirs, freqs, npoints = spectrum.shape
    tiles = npoints // TILE
    near = neighbours.shape[0]
    vmem = pl.BlockSpec(memory_space=pltpu.VMEM)
    return pl.pallas_call(
        functools.partial(local_kernel, ndirs),
        out_shape=jax.ShapeDtypeStruct((parts, 8, LANES), jnp.bfloat16),
        in_specs=[pl.BlockSpec(memory_space=pltpu.MemorySpace.HBM)] * 6,
        out_specs=vmem,
        scratch_shapes=[
            pltpu.VMEM((freqs, dirs, npoints), jnp.float32),
            pltpu.VMEM((near, npoints), jnp.int32),
            pltpu.VMEM((near, npoints), jnp.float32),
            pltpu.VMEM((near, npoints), jnp.float32),
            pltpu.VMEM((1, npoints), jnp.int32),
            pltpu.VMEM((1, npoints), jnp.int32),
            pltpu.SemaphoreType.DMA((6,)),
            pltpu.VMEM((dirs, 8, npoints), jnp.float32),
            pltpu.VMEM((TILE // LANES, dirs * freqs * tiles, LANES), jnp.float32),
            pltpu.VMEM((dirs * freqs * tiles, TILE), jnp.bfloat16),
            pltpu.VMEM((dirs, near, npoints), jnp.float32),
            pltpu.VMEM((1, npoints), jnp.float32),
            pltpu.VMEM((32 * tiles, TILE), jnp.float32),
            pltpu.VMEM((32 * tiles, TILE), jnp.bfloat16),
            pltpu.VMEM((TILE, TILE), jnp.bfloat16),
        ],
        compiler_params=pltpu.CompilerParams(vmem_limit_bytes=40 * 1024 * 1024),
        name="local_step",
    )(
        *(
            pltpu.with_memory_space_constraint(x, pltpu.MemorySpace.HBM)
            for x in (
                spectrum.transpose(1, 0, 2),
                neighbours,
                edge_angle,
                edge_coef,
                land_mask.reshape(1, npoints),
                space_order.reshape(1, npoints),
            )
        )
    )


def on_device(
    spectrum,
    neighbours,
    edge_angle,
    edge_coef,
    land_mask,
    dia_offsets,
    dia_coef,
    space_order,
    wind_speed,
    wind_dir,
):
    dirs, freqs, npoints = spectrum.shape
    nd, nf = lax.axis_size("dir"), lax.axis_size("freq")
    parts = nd * nf
    vmem = pl.BlockSpec(memory_space=pltpu.VMEM)
    smem = pl.BlockSpec(memory_space=pltpu.SMEM)
    blocks = local_call(
        nd * dirs, parts, spectrum, neighbours, edge_angle, edge_coef, land_mask, space_order
    )
    blocks = lax.all_to_all(blocks, ("dir", "freq"), split_axis=0, concat_axis=0, tiled=True)
    npts = npoints // parts
    done = pl.pallas_call(
        functools.partial(finish_kernel, nf),
        out_shape=jax.ShapeDtypeStruct((nd, NFREQ, 2 * npts), jnp.float32),
        in_specs=[smem, smem, vmem, vmem, vmem],
        out_specs=vmem,
        scratch_shapes=[
            pltpu.VMEM((2, nd + DSPAN, NFREQ + 16, LANES), jnp.float32),
            pltpu.VMEM((nd, NFREQ, LANES), jnp.float32),
            pltpu.VMEM((nd, LANES), jnp.float32),
        ],
        compiler_params=pltpu.CompilerParams(vmem_limit_bytes=40 * 1024 * 1024),
        name="finish_step",
    )(dia_offsets, dia_coef, wind_speed.reshape(1, npts), wind_dir.reshape(1, npts), blocks)
    done = done.reshape(nd, NFREQ, 2, npts).transpose(0, 2, 1, 3)
    return done.reshape(2 * nd, NFREQ, npts)


def solution(mesh):
    in_specs = (
        P("dir", "freq", None),
        P(),
        P(),
        P(),
        P(),
        P(),
        P(),
        P(),
        P(("dir", "freq")),
        P(("dir", "freq")),
    )
    out_specs = P(None, None, ("dir", "freq"))
    return jax.shard_map(
        on_device, mesh=mesh, in_specs=in_specs, out_specs=out_specs, check_vma=False
    )
```

time: 714 us -> 72.1 us (0.10)
  local copies, waits for them, and re-layouts: 558 us -> 1.78 us
  other arithmetic: 59.1 us -> 0.19 us
  waiting for transfers between devices: 40.2 us -> 0 us
  blocking collectives: 0 us -> 37 us
  starting transfers between devices: 35.6 us -> 0 us
  Pallas kernels: 0 us -> 33 us
  between operations: 15.2 us -> 0.05 us
    gather x13 -> x0, local copies, waits for them, and re-layouts: 478 us -> none  [the longest x12 418 us: propagate(): beside = jnp.take(masked, neighbours[k], axis=2)]
    all_to_all x0 -> x1, blocking collectives: none -> 37 us  [on_device(): lax.all_to_all(blocks, ('dir', 'freq'), split_axis=0, concat_axis=0, tile...]
    pallas_call x0 -> x2, Pallas kernels: none -> 33 us  [the longest x1 26.8 us: local_call(): pl.pallas_call(functools.partial(local_kernel, ndirs), out_shape=jax.Shap...]
    unnamed x24 -> x8, local copies, waits for them, and re-layouts: 32.6 us -> 0.02 us
    unnamed x1 -> x0, other arithmetic: 30.8 us -> none
    all_to_all x2 -> x0, waiting for transfers between devices: 20.6 us -> none  [the longest x1 14.4 us: on_device(): lax.all_to_all(reorder_points(payload, space_order), 'dir', split_axis=2,...]
    ppermute x8 -> x0, waiting for transfers between devices: 19.6 us -> none  [the longest x6 19.6 us: from_behind(): lax.ppermute(array, axis, [(i, (i + by) % count) for i in range(count)])]
    all_to_all x2 -> x0, starting transfers between devices: 17.9 us -> none  [the longest x1 12.1 us: on_device(): lax.all_to_all(reorder_points(payload, space_order), 'dir', split_axis=2,...]
  transfers between devices with their start and end apart: 10 -> 0, of which waited for: 6 -> 0; matrix products, arithmetic and copies ran while one was open for 63% -> 0% of each run, Pallas kernels for 0% -> 0%
where the time goes in v1:
time: 72.1 us; the launch traced here: 72 us
  blocking collectives  37 us (51%)
  Pallas kernels  33 us (46%)
  local copies, waits for them, and re-layouts  1.78 us (2%)
    all_to_all x1, blocking collectives, on_device(): lax.all_to_all(blocks, ('dir', 'freq'), split_axis=0, concat_axis=0, tile...  37 us
    pallas_call x1, Pallas kernels, local_call(): pl.pallas_call(functools.partial(local_kernel, ndirs), out_shape=jax.Shap...  26.8 us
    pallas_call x1, Pallas kernels, on_device(): pl.pallas_call(functools.partial(finish_kernel, nf), out_shape=jax.ShapeD...  6.25 us
    reshape x1, local copies, waits for them, and re-layouts, on_device(): return done.reshape(2 * nd, NFREQ, npts)  1.49 us

profile of v1, /device:TPU:1, one launch (start us, length us, event | category | flops | bytes accessed | tf_op | source)
XLA Modules:
  0.0 72.0 jit_solution(5062398572782149572)
XLA Ops:
  0.0 0.0 copy-start.3
  0.0 0.0 copy-start.2
  0.0 0.0 copy-start.1
  0.0 0.0 copy-start
  0.0 26.8 %local_step.1 = bf16[256,8,128]{2,1,0:T(8,128)(2,1)S(1)} custom-call(f32[6,2,8192]{2,1,0:T(2,128)} %bitcast.9, s32[6,8192]{1,0:T(8,128)} %nbr_at.1, f32[6,8192]{1,0:T(8,128)} %angle_at.1, f32[6,8192]{1,0:T(8,128)} %coef_at.1, s32[1,8192]{1,0:T(1,128)} %bitcast.10, s32[1,8192]{1,0:T(1,128)} %bitcast.11), custom_call_target="tpu_custom_call" | custom-call | tf_op jit(solution)/shard_map/local_step/pallas_call | solution.py:261
  26.8 37.0 %all_to_all.5.blocks = bf16[256,8,128]{2,1,0:T(8,128)(2,1)S(1)} all-to-all(bf16[256,8,128]{2,1,0:T(8,128)(2,1)S(1)} %local_step.1), channel_id=1, replica_groups=mesh['dir'=32,'freq'=8] {'dir','freq'}, dimensions={0} | all-to-all | bytes 1048576 | tf_op jit(solution)/shard_map/all_to_all | solution.py:320
  63.7 0.0 copy-done.3
  63.7 0.0 copy-done.2
  63.7 0.0 copy-done.1
  63.8 0.0 copy-done
  63.8 6.3 %finish_step.1 = f32[32,48,64]{2,1,0:T(8,128)S(1)} custom-call(s32[2,3]{1,0:T(2,128)S(1)} %copy-done, f32[3]{0:T(128)S(1)} %copy-done.1, f32[1,32]{1,0:T(1,128)S(1)} %bitcast.6, f32[1,32]{1,0:T(1,128)S(1)} %bitcast.7, bf16[256,8,128]{2,1,0:T(8,128)(2,1)S(1)} %all_to_all.5.blocks), custom_call_target="tpu_custom_call" | custom-call | tf_op jit(solution)/shard_map/finish_step/pallas_call | solution.py:322
  70.0 0.3 fusion
  70.3 0.2 pad_maximum_fusion
  70.5 1.5 %copy.19 = f32[64,48,32]{0,2,1:T(8,128)} copy(f32[64,48,32]{2,1,0:T(8,128)S(1)} %bitcast.8) | data formatting | bytes 786432 | tf_op jit(solution)/shard_map/reshape | solution.py:336
Async XLA Ops:
  0.0 63.7 %copy-start.3 = (f32[32]{0:T(128)S(1)}, f32[32]{0:T(128)}, u32[]{:S(2)}) copy-start(f32[32]{0:T(128)} %param.19) | copy-start | bytes 388
  0.0 63.7 %copy-start.2 = (f32[32]{0:T(128)S(1)}, f32[32]{0:T(128)}, u32[]{:S(2)}) copy-start(f32[32]{0:T(128)} %param.18) | copy-start | bytes 388
  0.0 63.7 %copy-start.1 = (f32[3]{0:T(128)S(1)}, f32[3]{0:T(128)}, u32[]{:S(2)}) copy-start(f32[3]{0:T(128)} %strength.1) | copy-start | bytes 40
  0.0 63.7 %copy-start = (s32[2,3]{1,0:T(2,128)S(1)}, s32[2,3]{1,0:T(2,128)}, u32[]{:S(2)}) copy-start(s32[2,3]{1,0:T(2,128)} %offsets.1) | copy-start | bytes 76

commit v2 on v1

--- a/solution.py
+++ b/solution.py
@@ -22,6 +22,7 @@
 
 LANES = 128
 TILE = 256
+STAGE, ADVECT, SWAP = 2, 4, 8
 CENTRE = 0.5
 
 
@@ -30,37 +31,40 @@
 
 
 def one_hot(low, ramp):
-    return jnp.where(ramp == low.astype(jnp.float32).astype(jnp.bfloat16), 1.0, 0.0).astype(jnp.bfloat16)
+    one, none = jnp.ones((), jnp.bfloat16), jnp.zeros((), jnp.bfloat16)
+    return jnp.where(ramp == low.astype(jnp.float32).astype(jnp.bfloat16), one, none)
 
 
 def local_kernel(
     ndirs, spec_at, nbr_at, angle_at, coef_at, mask_at, order_at, out,
-    spec, nbr, angle, coef, mask, order, arrived, field, pickf, pick, geom, wet, keepf, keep, ramp
+    spec, nbr, angle, coef, mask, order, arrived, field, pickf, pick, keepf, keep, ramp, *sums
 ):
-    dirs, freqs, npoints = 2, spec.shape[0], spec.shape[2]
-    pairs = [(spec_at, spec), (mask_at, mask), (angle_at, angle)]
-    pairs += [(coef_at, coef), (nbr_at, nbr), (order_at, order)]
+    freqs, dirs, npoints = spec.shape
+    tiles = npoints // TILE
+    near = nbr.shape[0]
+    first_dir = lax.axis_index("dir") * dirs
+    first_freq = lax.axis_index("freq") * freqs
+    pairs = [(spec_at, spec), (mask_at, mask), (nbr_at, nbr)]
+    pairs += [(angle_at, angle), (coef_at, coef), (order_at, order)]
     copies = [
         pltpu.make_async_copy(src, dst, arrived.at[n]) for n, (src, dst) in enumerate(pairs)
     ]
     for copy in copies:
         copy.start()
-    tiles = npoints // TILE
-    first_dir = lax.axis_index("dir") * dirs
-    first_freq = lax.axis_index("freq") * freqs
     sub = lax.broadcasted_iota(jnp.int32, (8, TILE), 0)
     lane = lax.broadcasted_iota(jnp.int32, (8, LANES), 1)
     speed = 0.5 / sigma_of(first_freq + sub)
     ramp[...] = lax.broadcasted_iota(jnp.int32, (TILE, TILE), 0).astype(jnp.float32).astype(jnp.bfloat16)
     pad = jnp.zeros((8 - freqs, TILE), jnp.float32)
-
-    for copy in copies[:4]:
+    for copy in copies[:2]:
         copy.wait()
 
+    def span(t):
+        return pl.ds(pl.multiple_of(t * TILE, TILE), TILE)
+
     def stage(t, carry):
-        at = pl.ds(pl.multiple_of(t * TILE, TILE), TILE)
+        at = span(t)
         wet_row = mask[:, at].astype(jnp.float32)
-        wet[:, at] = wet_row
         for i in range(dirs):
             rows = [spec[f, pl.ds(i, 1), at] for f in range(freqs)]
             value = jnp.concatenate(rows + [pad], axis=0)
@@ -69,91 +73,148 @@
             spot = pl.ds(i * freqs * tiles + t, freqs, stride=tiles)
             for c in range(TILE // LANES):
                 pickf[c, spot, :] = shown[:freqs, c * LANES : (c + 1) * LANES]
-            theta = (2.0 * math.pi / ndirs) * (first_dir + i).astype(jnp.float32)
-            bearing = jnp.cos(theta - angle[:, at])
-            geom[i, :, at] = coef[:, at] * jnp.maximum(bearing, 0.0)
         return carry
 
-    lax.fori_loop(0, tiles, stage, 0)
+    lax.fori_loop(0, tiles, stage, 0, unroll=STAGE)
     for c in range(TILE // LANES):
         pick[:, c * LANES : (c + 1) * LANES] = pickf[c].astype(jnp.bfloat16)
+    for copy in copies[2:5]:
+        copy.wait()
+
+    def split(index):
+        low = jnp.bitwise_and(index, TILE - 1)
+        high = jnp.broadcast_to(jnp.right_shift(index, 8), (8, TILE))
+        return one_hot(low, ramp[...]), high
+
+    def issue(job, table, accs, index, chunk):
+        unit, slot = job % 2, job // 2 % 2
+        hot, high = split(index)
+        pltpu.matmul_push_rhs(hot, slot, unit)
+        for c, acc in enumerate(accs[unit][slot]):
+            rows = table[c * chunk : (c + 1) * chunk, :]
+            pltpu.matmul_acc_lhs(acc, rows, load_staged_rhs=slot if c == 0 else None)
+        return high
 
     groups = tiles // 8
-
-    copies[4].wait()
-
-    def advect(t, carry):
-        at = pl.ds(pl.multiple_of(t * TILE, TILE), TILE)
-        total = [jnp.zeros((8, TILE), jnp.float32) for _ in range(dirs * freqs)]
-        weight = [jnp.zeros((1, TILE), jnp.float32) for _ in range(dirs)]
-        for k in range(nbr.shape[0]):
-            index = nbr[k : k + 1, at]
-            low = jnp.bitwise_and(index, TILE - 1)
-            high = jnp.broadcast_to(jnp.right_shift(index, 8), (8, TILE))
-            found = jnp.dot(pick[...], one_hot(low, ramp[...]), preferred_element_type=jnp.float32)
+    chunk = 3 * tiles
+    count = dirs * freqs // 3
+    accs = [[sums[(u * 2 + v) * count : (u * 2 + v + 1) * count] for v in range(2)] for u in range(2)]
+
+    def advect(step, carry):
+        jobs = [(u, k) for u in range(ADVECT) for k in range(near)]
+        highs = {}
+
+        def start(n):
+            u, k = jobs[n]
+            highs[n] = issue(n, pick, accs, nbr[k : k + 1, span(step * ADVECT + u)], chunk)
+
+        start(0)
+        start(1)
+        for n, (u, k) in enumerate(jobs):
+            t = step * ADVECT + u
+            at = span(t)
+            if k == 0:
+                total = [jnp.zeros((8, TILE), jnp.float32) for _ in range(dirs * freqs)]
+                geom = []
+                for i in range(dirs):
+                    theta = (2.0 * math.pi / ndirs) * (first_dir + i).astype(jnp.float32)
+                    bearing = jnp.cos(theta - angle[:, at])
+                    geom.append(coef[:, at] * jnp.maximum(bearing, 0.0))
+            high = highs.pop(n)
             match = [high == sub + 8 * h for h in range(groups)]
-            for i in range(dirs):
-                row = geom[i, k : k + 1, at]
-                weight[i] = weight[i] + row
-                for f in range(freqs):
-                    r = i * freqs + f
+            rows = [geom[i][k : k + 1] for i in range(dirs)]
+            unit, slot = n % 2, n // 2 % 2
+            for c, acc in enumerate(accs[unit][slot]):
+                found = pltpu.matmul_pop(acc)
+                for x in range(3):
+                    r = c * 3 + x
                     chosen = jnp.zeros((8, TILE), jnp.float32)
                     for h in range(groups):
-                        start = r * tiles + 8 * h
-                        chosen = jnp.where(match[h], found[start : start + 8], chosen)
-                    total[r] = total[r] + row * chosen
-        wet_row = wet[:, at]
-        kept, rest = [], []
-        for i in range(dirs):
-            value = field[i, :, at]
-            rows = [
-                jnp.sum(total[i * freqs + f], axis=0, keepdims=True) for f in range(freqs)
-            ]
-            inflow = jnp.concatenate(rows + [pad], axis=0)
-            moved = value + speed * (inflow + weight[i] * (CENTRE - value))
-            old = value.astype(jnp.bfloat16).astype(jnp.float32)
-            kept.append(wet_row * old)
-            rest.append(wet_row * (moved - old))
-        for g, part in enumerate(kept + rest):
-            keepf[pl.ds(pl.multiple_of(t * 32, 32) + 8 * g, 8), :] = part
+                        begin = x * tiles + 8 * h
+                        chosen = jnp.where(match[h], found[begin : begin + 8], chosen)
+                    total[r] = total[r] + rows[r // freqs] * chosen
+            if n + 2 < len(jobs):
+                start(n + 2)
+            if k == near - 1:
+                wet_row = mask[:, at].astype(jnp.float32)
+                kept, rest = [], []
+                for i in range(dirs):
+                    value = field[i, :, at]
+                    weight = jnp.sum(geom[i], axis=0, keepdims=True)
+                    lines = [
+                        jnp.sum(total[i * freqs + f], axis=0, keepdims=True) for f in range(freqs)
+                    ]
+                    inflow = jnp.concatenate(lines + [pad], axis=0)
+                    moved = value + speed * (inflow + weight * (CENTRE - value))
+                    old = value.astype(jnp.bfloat16).astype(jnp.float32)
+                    kept.append((wet_row * old)[:freqs])
+                    rest.append((wet_row * (moved - old))[:freqs])
+                width = 2 * dirs * freqs
+                spot = pl.ds(pl.multiple_of(t * width, 8), width)
+                keepf[spot, :] = jnp.concatenate(kept + rest, axis=0)
         return carry
 
-    lax.fori_loop(0, tiles, advect, 0, unroll=4)
+    lax.fori_loop(0, tiles // ADVECT, advect, 0)
     keep[...] = keepf[...].astype(jnp.bfloat16)
-
     copies[5].wait()
-
-    def swap(t, carry):
-        at = pl.ds(pl.multiple_of(t * TILE, TILE), TILE)
-        index = order[:, at]
-        low = jnp.bitwise_and(index, TILE - 1)
-        high = jnp.broadcast_to(jnp.right_shift(index, 8), (8, TILE))
-        found = jnp.dot(keep[...], one_hot(low, ramp[...]), preferred_element_type=jnp.float32)
-        part = [jnp.zeros((8, TILE), jnp.float32) for _ in range(4)]
-        for h in range(tiles):
-            match = high == h
-            for g in range(4):
-                start = 32 * h + 8 * g
-                part[g] = jnp.where(match, found[start : start + 8], part[g])
-        for c in range(TILE // LANES):
-            v = [x[:, c * LANES : (c + 1) * LANES] for x in part]
-            left = lane < 64
-            w0 = jnp.where(left, v[0], pltpu.roll(v[2], 64, 1))
-            w2 = jnp.where(left, pltpu.roll(v[0], 64, 1), v[2])
-            w1 = jnp.where(left, v[1], pltpu.roll(v[3], 64, 1))
-            w3 = jnp.where(left, pltpu.roll(v[1], 64, 1), v[3])
-            even = jnp.bitwise_and(lane, 32) == 0
-            blocks = [
-                jnp.where(even, w0, pltpu.roll(w1, 32, 1)),
-                jnp.where(even, pltpu.roll(w0, 96, 1), w1),
-                jnp.where(even, w2, pltpu.roll(w3, 32, 1)),
-                jnp.where(even, pltpu.roll(w2, 96, 1), w3),
-            ]
-            for b in range(4):
-                out[t * 8 + c * 4 + b] = blocks[b].astype(jnp.bfloat16)
+    width = 2 * dirs * freqs
+
+    def swap(step, carry):
+        jobs = list(range(SWAP))
+        highs = {}
+        hots = {}
+        accs = [[*sums[: 2 * count]], [*sums[2 * count :]]]
+
+        def push(n):
+            hots[n], highs[n] = split(order[:, span(step * SWAP + n)])
+            pltpu.matmul_push_rhs(hots[n], n // 2 % 2, n % 2)
+
+        def multiply(n, c):
+            rows = keep[c * chunk : (c + 1) * chunk, :]
+            slot = n // 2 % 2 if c == 0 else None
+            pltpu.matmul_acc_lhs(accs[n % 2][c], rows, load_staged_rhs=slot)
+
+        for n in jobs[:2]:
+            push(n)
+            for c in range(2 * count):
+                multiply(n, c)
+        for n in jobs:
+            high = highs.pop(n)
+            part = [jnp.zeros((8, TILE), jnp.float32) for _ in range(width // 8)]
+            if n + 2 < len(jobs):
+                push(n + 2)
+            for c in range(2 * count):
+                found = pltpu.matmul_pop(accs[n % 2][c])
+                if n + 2 < len(jobs):
+                    multiply(n + 2, c)
+                for x in range(chunk // width):
+                    match = high == c * (chunk // width) + x
+                    for g in range(width // 8):
+                        begin = x * width + 8 * g
+                        part[g] = jnp.where(match, found[begin : begin + 8], part[g])
+            whole = jnp.concatenate(part, axis=0)
+            whole = [whole[g * freqs : (g + 1) * freqs] for g in range(2 * dirs)]
+            whole = [jnp.concatenate([x, pad], axis=0) for x in whole]
+            for c in range(TILE // LANES):
+                v = [x[:, c * LANES : (c + 1) * LANES] for x in whole]
+                left = lane < 64
+                w0 = jnp.where(left, v[0], pltpu.roll(v[2], 64, 1))
+                w2 = jnp.where(left, pltpu.roll(v[0], 64, 1), v[2])
+                w1 = jnp.where(left, v[1], pltpu.roll(v[3], 64, 1))
+                w3 = jnp.where(left, pltpu.roll(v[1], 64, 1), v[3])
+                even = jnp.bitwise_and(lane, 32) == 0
+                blocks = [
+                    jnp.where(even, w0, pltpu.roll(w1, 32, 1)),
+                    jnp.where(even, pltpu.roll(w0, 96, 1), w1),
+                    jnp.where(even, w2, pltpu.roll(w3, 32, 1)),
+                    jnp.where(even, pltpu.roll(w2, 96, 1), w3),
+                ]
+                for b in range(4):
+                    spot = (step * SWAP + n) * 8 + c * 4 + b
+                    out[spot] = blocks[b].astype(jnp.bfloat16)
         return carry
 
-    lax.fori_loop(0, tiles, swap, 0, unroll=4)
+    lax.fori_loop(0, tiles // SWAP, swap, 0)
 
 
 def finish_kernel(
@@ -251,6 +312,16 @@
     lax.fori_loop(0, pairs, grow, 0)
 
 
+def local_scoped(ndirs, *refs):
+    freqs, dirs, npoints = refs[0].shape
+    sums = [
+        pltpu.ACC(unit)((3 * npoints // TILE, TILE), jnp.float32)
+        for unit in range(2)
+        for _ in range(2 * dirs * freqs // 3)
+    ]
+    pl.run_scoped(lambda *sums: local_kernel(ndirs, *refs, *sums), *sums)
+
+
 def local_call(
     ndirs, parts, spectrum, neighbours, edge_angle, edge_coef, land_mask, space_order
 ):
@@ -259,7 +330,7 @@
     near = neighbours.shape[0]
     vmem = pl.BlockSpec(memory_space=pltpu.VMEM)
     return pl.pallas_call(
-        functools.partial(local_kernel, ndirs),
+        functools.partial(local_scoped, ndirs),
         out_shape=jax.ShapeDtypeStruct((parts, 8, LANES), jnp.bfloat16),
         in_specs=[pl.BlockSpec(memory_space=pltpu.MemorySpace.HBM)] * 6,
         out_specs=vmem,
@@ -274,10 +345,8 @@
             pltpu.VMEM((dirs, 8, npoints), jnp.float32),
             pltpu.VMEM((TILE // LANES, dirs * freqs * tiles, LANES), jnp.float32),
             pltpu.VMEM((dirs * freqs * tiles, TILE), jnp.bfloat16),
-            pltpu.VMEM((dirs, near, npoints), jnp.float32),
-            pltpu.VMEM((1, npoints), jnp.float32),
-            pltpu.VMEM((32 * tiles, TILE), jnp.float32),
-            pltpu.VMEM((32 * tiles, TILE), jnp.bfloat16),
+            pltpu.VMEM((2 * dirs * freqs * tiles, TILE), jnp.float32),
+            pltpu.VMEM((2 * dirs * freqs * tiles, TILE), jnp.bfloat16),
             pltpu.VMEM((TILE, TILE), jnp.bfloat16),
         ],
         compiler_params=pltpu.CompilerParams(vmem_limit_bytes=40 * 1024 * 1024),

time: 72.1 us -> 63.8 us (0.88)
  Pallas kernels: 33 us -> 24.8 us
    pallas_call x1, Pallas kernels: 26.8 us -> 18.5 us  [local_call(): pl.pallas_call(functools.partial(local_scoped, ndirs), out_shape=jax.Shap...]
where the time goes in v2:
time: 63.8 us; the launch traced here: 63.7 us
  blocking collectives  36.9 us (58%)
  Pallas kernels  24.8 us (39%)
  local copies, waits for them, and re-layouts  1.78 us (3%)
    all_to_all x1, blocking collectives, on_device(): lax.all_to_all(blocks, ('dir', 'freq'), split_axis=0, concat_axis=0, tile...  36.9 us
    pallas_call x1, Pallas kernels, local_call(): pl.pallas_call(functools.partial(local_scoped, ndirs), out_shape=jax.Shap...  18.5 us
    pallas_call x1, Pallas kernels, on_device(): pl.pallas_call(functools.partial(finish_kernel, nf), out_shape=jax.ShapeD...  6.25 us
    reshape x1, local copies, waits for them, and re-layouts, on_device(): return done.reshape(2 * nd, NFREQ, npts)  1.49 us

profile of v2, /device:TPU:1, one launch (start us, length us, event | category | flops | bytes accessed | tf_op | source)
XLA Modules:
  0.0 63.7 jit_solution(16805693615759935932)
XLA Ops:
  0.0 0.0 copy-start.3
  0.0 0.0 copy-start.2
  0.0 0.0 copy-start.1
  0.0 0.0 copy-start
  0.0 18.5 %local_step.1 = bf16[256,8,128]{2,1,0:T(8,128)(2,1)S(1)} custom-call(f32[6,2,8192]{2,1,0:T(2,128)} %bitcast.9, s32[6,8192]{1,0:T(8,128)} %refs_1_.1, f32[6,8192]{1,0:T(8,128)} %refs_2_.1, f32[6,8192]{1,0:T(8,128)} %refs_3_.1, s32[1,8192]{1,0:T(1,128)} %bitcast.10, s32[1,8192]{1,0:T(1,128)} %bitcast.11), custom_call_target="tpu_custom_call" | custom-call | tf_op jit(solution)/shard_map/local_step/pallas_call | solution.py:332
  18.5 36.9 %all_to_all.5.blocks = bf16[256,8,128]{2,1,0:T(8,128)(2,1)S(1)} all-to-all(bf16[256,8,128]{2,1,0:T(8,128)(2,1)S(1)} %local_step.1), channel_id=1, replica_groups=mesh['dir'=32,'freq'=8] {'dir','freq'}, dimensions={0} | all-to-all | bytes 1048576 | tf_op jit(solution)/shard_map/all_to_all | solution.py:389
  55.5 0.0 copy-done.3
  55.5 0.0 copy-done.2
  55.5 0.0 copy-done.1
  55.5 0.0 copy-done
  55.5 6.3 %finish_step.1 = f32[32,48,64]{2,1,0:T(8,128)S(1)} custom-call(s32[2,3]{1,0:T(2,128)S(1)} %copy-done, f32[3]{0:T(128)S(1)} %copy-done.1, f32[1,32]{1,0:T(1,128)S(1)} %bitcast.6, f32[1,32]{1,0:T(1,128)S(1)} %bitcast.7, bf16[256,8,128]{2,1,0:T(8,128)(2,1)S(1)} %all_to_all.5.blocks), custom_call_target="tpu_custom_call" | custom-call | tf_op jit(solution)/shard_map/finish_step/pallas_call | solution.py:391
  61.8 0.3 fusion
  62.0 0.2 pad_maximum_fusion
  62.2 1.5 %copy.19 = f32[64,48,32]{0,2,1:T(8,128)} copy(f32[64,48,32]{2,1,0:T(8,128)S(1)} %bitcast.8) | data formatting | bytes 786432 | tf_op jit(solution)/shard_map/reshape | solution.py:405
Async XLA Ops:
  0.0 55.5 %copy-start.3 = (f32[32]{0:T(128)S(1)}, f32[32]{0:T(128)}, u32[]{:S(2)}) copy-start(f32[32]{0:T(128)} %param.19) | copy-start | bytes 388
  0.0 55.5 %copy-start.2 = (f32[32]{0:T(128)S(1)}, f32[32]{0:T(128)}, u32[]{:S(2)}) copy-start(f32[32]{0:T(128)} %param.18) | copy-start | bytes 388
  0.0 55.5 %copy-start.1 = (f32[3]{0:T(128)S(1)}, f32[3]{0:T(128)}, u32[]{:S(2)}) copy-start(f32[3]{0:T(128)} %strength.1) | copy-start | bytes 40
  0.0 55.5 %copy-start = (s32[2,3]{1,0:T(2,128)S(1)}, s32[2,3]{1,0:T(2,128)}, u32[]{:S(2)}) copy-start(s32[2,3]{1,0:T(2,128)} %offsets.1) | copy-start | bytes 76

commit v3 on v2

--- a/solution.py
+++ b/solution.py
@@ -22,7 +22,8 @@
 
 LANES = 128
 TILE = 256
-STAGE, ADVECT, SWAP = 2, 4, 8
+WIDEN, UNPACK, TRANSFER, GROW = 8, 8, 4, 8
+STAGE, ADVECT, SWAP = 2, 8, 8
 CENTRE = 0.5
 
 
@@ -97,6 +98,7 @@
 
     groups = tiles // 8
     chunk = 3 * tiles
+    width = 2 * dirs * freqs
     count = dirs * freqs // 3
     accs = [[sums[(u * 2 + v) * count : (u * 2 + v + 1) * count] for v in range(2)] for u in range(2)]
 
@@ -137,7 +139,6 @@
                 start(n + 2)
             if k == near - 1:
                 wet_row = mask[:, at].astype(jnp.float32)
-                kept, rest = [], []
                 for i in range(dirs):
                     value = field[i, :, at]
                     weight = jnp.sum(geom[i], axis=0, keepdims=True)
@@ -147,17 +148,21 @@
                     inflow = jnp.concatenate(lines + [pad], axis=0)
                     moved = value + speed * (inflow + weight * (CENTRE - value))
                     old = value.astype(jnp.bfloat16).astype(jnp.float32)
-                    kept.append((wet_row * old)[:freqs])
-                    rest.append((wet_row * (moved - old))[:freqs])
-                width = 2 * dirs * freqs
-                spot = pl.ds(pl.multiple_of(t * width, 8), width)
-                keepf[spot, :] = jnp.concatenate(kept + rest, axis=0)
+                    for n, part in enumerate((wet_row * old, wet_row * (moved - old))):
+                        spot = pl.ds(t * width + i * 2 + n, freqs, stride=2 * dirs)
+                        for c in range(TILE // LANES):
+                            keepf[c, spot, :] = part[:freqs, c * LANES : (c + 1) * LANES]
         return carry
 
     lax.fori_loop(0, tiles // ADVECT, advect, 0)
-    keep[...] = keepf[...].astype(jnp.bfloat16)
+    for c in range(TILE // LANES):
+        keep[:, c * LANES : (c + 1) * LANES] = keepf[c].astype(jnp.bfloat16)
     copies[5].wait()
-    width = 2 * dirs * freqs
+
+    row = sub[:, :LANES]
+    outer = jnp.right_shift(row, 2) == jnp.right_shift(lane, 6)
+    inner = jnp.bitwise_and(row, 2) == jnp.bitwise_and(jnp.right_shift(lane, 4), 2)
+    first = jnp.bitwise_and(row, 2) == 0
 
     def swap(step, carry):
         jobs = list(range(SWAP))
@@ -192,124 +197,139 @@
                     for g in range(width // 8):
                         begin = x * width + 8 * g
                         part[g] = jnp.where(match, found[begin : begin + 8], part[g])
-            whole = jnp.concatenate(part, axis=0)
-            whole = [whole[g * freqs : (g + 1) * freqs] for g in range(2 * dirs)]
-            whole = [jnp.concatenate([x, pad], axis=0) for x in whole]
-            for c in range(TILE // LANES):
-                v = [x[:, c * LANES : (c + 1) * LANES] for x in whole]
-                left = lane < 64
-                w0 = jnp.where(left, v[0], pltpu.roll(v[2], 64, 1))
-                w2 = jnp.where(left, pltpu.roll(v[0], 64, 1), v[2])
-                w1 = jnp.where(left, v[1], pltpu.roll(v[3], 64, 1))
-                w3 = jnp.where(left, pltpu.roll(v[1], 64, 1), v[3])
-                even = jnp.bitwise_and(lane, 32) == 0
-                blocks = [
-                    jnp.where(even, w0, pltpu.roll(w1, 32, 1)),
-                    jnp.where(even, pltpu.roll(w0, 96, 1), w1),
-                    jnp.where(even, w2, pltpu.roll(w3, 32, 1)),
-                    jnp.where(even, pltpu.roll(w2, 96, 1), w3),
-                ]
-                for b in range(4):
-                    spot = (step * SWAP + n) * 8 + c * 4 + b
-                    out[spot] = blocks[b].astype(jnp.bfloat16)
+            for g, whole in enumerate(part):
+                for c in range(TILE // LANES):
+                    x = whole[:, c * LANES : (c + 1) * LANES]
+                    x = jnp.where(outer, x, pltpu.roll(pltpu.roll(x, 4, 0), 64, 1))
+                    after = pltpu.roll(pltpu.roll(x, 6, 0), 32, 1)
+                    before = pltpu.roll(pltpu.roll(x, 2, 0), 96, 1)
+                    x = jnp.where(inner, x, jnp.where(first, after, before)).astype(jnp.bfloat16)
+                    for b in range(4):
+                        spot = ((step * SWAP + n) * 8 + c * 4 + b) * (width // 8) + g
+                        out[spot] = x[2 * b : 2 * b + 2]
         return carry
 
     lax.fori_loop(0, tiles // SWAP, swap, 0)
 
 
 def finish_kernel(
-    freq_blocks, offsets, strength, wind_speed, wind_dir, blocks, out, table, relaid, rows
+    ndirs, offsets, strength, wind_speed, wind_dir, blocks, out, table, relaid, rows, lines
 ):
-    nblocks, _, _ = blocks.shape
-    pairs = nblocks // freq_blocks
+    pairs = ndirs // 2
     reach = DSPAN // 2
-    freqs = NFREQ // freq_blocks
-    low_pad = 8
-    lane = lax.broadcasted_iota(jnp.int32, (NFREQ, LANES), 1)
-    first = lane < 32
-    half = lane < 64
-    ndirs = 2 * pairs
-    npts = 32
-
-    edge = jnp.zeros((8, LANES), jnp.float32)
-    for parity in range(2):
-        for s in range(pairs + 2 * reach):
-            table[parity, s, 0:8] = edge
-            table[parity, s, low_pad + NFREQ : low_pad + NFREQ + 8] = edge
+    lots = table.shape[2] - 2
+    sub = lax.broadcasted_iota(jnp.int32, (8, LANES), 0)
+    lane = lax.broadcasted_iota(jnp.int32, (8, LANES), 1)
+    second = jnp.bitwise_and(lane, 32) == 0
+    first = lane < 64
+    per = 8 * lots
+
+    def turn(x):
+        return jnp.where(second, pltpu.roll(x, LANES - 32, 1), pltpu.roll(x, 32, 1))
+
+    def widen(s, carry):
+        piece = blocks[pl.ds(s * per, per)].astype(jnp.float32)
+        spot = pl.ds(pl.multiple_of(s * 2 * per, 2 * per), 2 * per)
+        lines[spot, :] = piece.reshape(2 * per, LANES)
+        return carry
+
+    lax.fori_loop(0, pairs, widen, 0, unroll=WIDEN)
 
     def unpack(s, carry):
-        for b in range(freq_blocks):
-            piece = blocks[s * freq_blocks + b].astype(jnp.float32)
-            table[0, s + reach, low_pad + b * freqs : low_pad + (b + 1) * freqs] = piece[:freqs]
-        body = table[0, s + reach, low_pad : low_pad + NFREQ]
-        turned = jnp.where(first, pltpu.roll(body, LANES - 32, 1), pltpu.roll(body, 32, 1))
-        table[1, s + reach, low_pad : low_pad + NFREQ] = turned
-        return carry
-
-    lax.fori_loop(0, pairs, unpack, 0)
-    for parity in range(2):
-        for s in range(reach):
-            table[parity, s] = table[parity, s + pairs]
-            table[parity, s + pairs + reach] = table[parity, s + reach]
+        for b in range(lots):
+            begin = s * 2 * per + 2 * b
+            old = lines[pl.ds(begin, 8, stride=2 * lots), :]
+            relaid[b, s] = lines[pl.ds(begin + 1, 8, stride=2 * lots), :]
+            other = pltpu.roll(old, 64, 1)
+            forms = ((old, turn(old)), (other, turn(other)))
+            for i in range(2):
+                for j in range(2):
+                    table[i, j, b + 1, s + reach] = forms[i][j]
+                    if b == 0:
+                        shifted = jnp.where(sub == 7, 0.0, pltpu.roll(forms[i][j], 7, 0))
+                        table[i, j, lots + 1, s + reach] = shifted
+                    if b == lots - 1:
+                        shifted = jnp.where(sub == 0, 0.0, pltpu.roll(forms[i][j], 1, 0))
+                        table[i, j, 0, s + reach] = shifted
+        return carry
+
+    lax.fori_loop(0, pairs, unpack, 0, unroll=UNPACK)
+    for i in range(2):
+        for j in range(2):
+            for b in range(lots + 2):
+                for s in range(reach):
+                    table[i, j, b, s] = table[i, j, b, s + pairs]
+                    table[i, j, b, s + pairs + reach] = table[i, j, b, s + reach]
+
+    shapes = []
+    for q in range(strength.shape[0]):
+        d, m, c = offsets[0, q], offsets[1, q], strength[q]
+        at = [jnp.right_shift(m + x, 1) + 1 for x in range(2)]
+        to = [jnp.right_shift(d + x, 1) + reach for x in range(2)]
+        back_at = [jnp.right_shift(x - m, 1) + 1 for x in range(2)]
+        back_to = [jnp.right_shift(x - d, 1) + reach for x in range(2)]
+        odd = (jnp.bitwise_and(m, 1), jnp.bitwise_and(d, 1))
+        shapes.append((odd, at, to, back_at, back_to, c))
 
     def transfer(s, carry):
-        total = carry
-        body = table[0, s + reach, low_pad : low_pad + NFREQ]
-        moved = body + pltpu.roll(body, 64, 1)
-        change = jnp.zeros((NFREQ, LANES), jnp.float32)
-        for q in range(strength.shape[0]):
-            d = offsets[0, q]
-            m = offsets[1, q]
-            odd = jnp.bitwise_and(d, 1)
-
-            def shifted(by, start):
-                near = s + reach + jnp.right_shift(by, 1)
-                far = s + reach + jnp.right_shift(by + 1, 1)
-                at = pl.ds(low_pad + start, NFREQ)
-                return jnp.where(first, table[odd, near, at], table[odd, far, at])
-
-            upper = shifted(d, m)
-            lower = shifted(-d, -m)
-            delta = body * body * (upper + lower) - 2.0 * body * upper * lower
-            change = change + strength[q] * delta
-        value = moved + DT_NL * change
-        relaid[s] = value
-        return total + value
-
-    total = lax.fori_loop(0, pairs, transfer, jnp.zeros((NFREQ, LANES), jnp.float32))
-
-    sigma = sigma_of(lax.broadcasted_iota(jnp.int32, (NFREQ, LANES), 0))
+        total = list(carry)
+        for b in range(lots):
+            body = table[0, 0, b + 1, s + reach]
+            plain = jnp.zeros((8, LANES), jnp.float32)
+            cross = jnp.zeros((8, LANES), jnp.float32)
+            for odd, at, to, back_at, back_to, c in shapes:
+
+                def shifted(at, to):
+                    got = [[table[odd[0], odd[1], b + x, s + y] for y in to] for x in at]
+                    got = [jnp.where(second, x[0], x[1]) for x in got]
+                    return jnp.where(first, got[0], got[1])
+
+                upper, lower = shifted(at, to), shifted(back_at, back_to)
+                plain = plain + c * (upper + lower)
+                cross = cross + (2.0 * c) * (upper * lower)
+            value = body + relaid[b, s] + DT_NL * (body * (body * plain - cross))
+            relaid[b, s] = value
+            total[b] = total[b] + value
+        return tuple(total)
+
+    empty = jnp.zeros((8, LANES), jnp.float32)
+    total = lax.fori_loop(0, pairs, transfer, (empty,) * lots, unroll=TRANSFER)
+
+    half = jnp.right_shift(lane, 6)
+    sigma = [sigma_of(sub * (2 * lots) + 2 * b + half) for b in range(lots)]
     weight = 1.0 / (ndirs * NFREQ)
 
-    def over_dirs(x):
-        x = jnp.sum(x, axis=0, keepdims=True)
+    def over_all(terms):
+        x = jnp.sum(sum(terms), axis=0, keepdims=True)
         x = jnp.broadcast_to(x, (8, LANES))
-        lane8 = lane[:8]
-        x = x + jnp.where(lane8 < 32, pltpu.roll(x, LANES - 32, 1), pltpu.roll(x, 32, 1))
-        return x[:1]
-
-    etot = over_dirs(total) * weight
-    inverse = over_dirs(total / sigma) * weight
+        x = x + pltpu.roll(x, 64, 1)
+        return x + pltpu.roll(x, 32, 1)
+
+    etot = over_all(total) * weight
+    inverse = over_all([x / y for x, y in zip(total, sigma)]) * weight
     msig = jnp.clip(etot / jnp.maximum(inverse, INV_FLOOR), SIG_LO, SIG_HI)
     steep = etot * (msig * msig * msig * msig) / APM
-    ratio = sigma / msig
-    rate = CDS * (ratio * ratio) * msig * (steep * steep)
-    damp = 1.0 / (1.0 + rate)
-    wind = jnp.concatenate([wind_speed[...]] * 4, axis=1) * sigma
+    rate = [CDS * ((x / msig) * (x / msig)) * msig * (steep * steep) for x in sigma]
+    damp = [1.0 / (1.0 + x) for x in rate]
+    speed = jnp.concatenate([wind_speed[...]] * 4, axis=1)
+    wind = [speed * x for x in sigma]
+    push = [BETA * x for x in sigma]
     towards = jnp.concatenate([wind_dir[...]] * 4, axis=1)
     step = lax.broadcasted_iota(jnp.int32, (pairs, LANES), 0) * 2 + jnp.bitwise_and(
         jnp.right_shift(lax.broadcasted_iota(jnp.int32, (pairs, LANES), 1), 5), 1
     )
     rows[...] = jnp.cos((2.0 * math.pi / ndirs) * step.astype(jnp.float32) - towards)
-    push = BETA * sigma
 
     def grow(s, carry):
-        growth = push * jnp.maximum(wind * rows[pl.ds(s, 1), :] - 1.0, 0.0)
-        value = relaid[s] * (1.0 + growth) * damp
-        out[s] = value[:, :64]
-        return carry
-
-    lax.fori_loop(0, pairs, grow, 0)
+        along = rows[pl.ds(s, 1), :]
+        for b in range(lots):
+            growth = push[b] * jnp.maximum(wind[b] * along - 1.0, 0.0)
+            value = relaid[b, s] * (1.0 + growth) * damp[b]
+            out[s, pl.ds(2 * b, 8, stride=2 * lots), :] = value
+            out[s, pl.ds(2 * b + 1, 8, stride=2 * lots), :] = pltpu.roll(value, 64, 1)
+        return carry
+
+    lax.fori_loop(0, pairs, grow, 0, unroll=GROW)
 
 
 def local_scoped(ndirs, *refs):
@@ -331,7 +351,7 @@
     vmem = pl.BlockSpec(memory_space=pltpu.VMEM)
     return pl.pallas_call(
         functools.partial(local_scoped, ndirs),
-        out_shape=jax.ShapeDtypeStruct((parts, 8, LANES), jnp.bfloat16),
+        out_shape=jax.ShapeDtypeStruct((parts * dirs * freqs // 4, 2, LANES), jnp.bfloat16),
         in_specs=[pl.BlockSpec(memory_space=pltpu.MemorySpace.HBM)] * 6,
         out_specs=vmem,
         scratch_shapes=[
@@ -345,7 +365,7 @@
             pltpu.VMEM((dirs, 8, npoints), jnp.float32),
             pltpu.VMEM((TILE // LANES, dirs * freqs * tiles, LANES), jnp.float32),
             pltpu.VMEM((dirs * freqs * tiles, TILE), jnp.bfloat16),
-            pltpu.VMEM((2 * dirs * freqs * tiles, TILE), jnp.float32),
+            pltpu.VMEM((TILE // LANES, 2 * dirs * freqs * tiles, LANES), jnp.float32),
             pltpu.VMEM((2 * dirs * freqs * tiles, TILE), jnp.bfloat16),
             pltpu.VMEM((TILE, TILE), jnp.bfloat16),
         ],
@@ -366,6 +386,26 @@
     )
 
 
+def finish_call(ndirs, nd, nf, dia_offsets, dia_coef, wind_speed, wind_dir, blocks):
+    vmem = pl.BlockSpec(memory_space=pltpu.VMEM)
+    smem = pl.BlockSpec(memory_space=pltpu.SMEM)
+    lots = blocks.shape[0] // (nd * nf)
+    return pl.pallas_call(
+        functools.partial(finish_kernel, ndirs),
+        out_shape=jax.ShapeDtypeStruct((nd, NFREQ, LANES), jnp.float32),
+        in_specs=[smem, smem, vmem, vmem, vmem],
+        out_specs=vmem,
+        scratch_shapes=[
+            pltpu.VMEM((2, 2, lots + 2, nd + DSPAN, nf, LANES), jnp.float32),
+            pltpu.VMEM((lots, nd, nf, LANES), jnp.float32),
+            pltpu.VMEM((nd, LANES), jnp.float32),
+            pltpu.VMEM((2 * nf * lots * nd, LANES), jnp.float32),
+        ],
+        compiler_params=pltpu.CompilerParams(vmem_limit_bytes=40 * 1024 * 1024),
+        name="finish_step",
+    )(dia_offsets, dia_coef, wind_speed, wind_dir, blocks)
+
+
 def on_device(
     spectrum,
     neighbours,
@@ -381,27 +421,16 @@
     dirs, freqs, npoints = spectrum.shape
     nd, nf = lax.axis_size("dir"), lax.axis_size("freq")
     parts = nd * nf
-    vmem = pl.BlockSpec(memory_space=pltpu.VMEM)
-    smem = pl.BlockSpec(memory_space=pltpu.SMEM)
     blocks = local_call(
         nd * dirs, parts, spectrum, neighbours, edge_angle, edge_coef, land_mask, space_order
     )
     blocks = lax.all_to_all(blocks, ("dir", "freq"), split_axis=0, concat_axis=0, tiled=True)
     npts = npoints // parts
-    done = pl.pallas_call(
-        functools.partial(finish_kernel, nf),
-        out_shape=jax.ShapeDtypeStruct((nd, NFREQ, 2 * npts), jnp.float32),
-        in_specs=[smem, smem, vmem, vmem, vmem],
-        out_specs=vmem,
-        scratch_shapes=[
-            pltpu.VMEM((2, nd + DSPAN, NFREQ + 16, LANES), jnp.float32),
-            pltpu.VMEM((nd, NFREQ, LANES), jnp.float32),
-            pltpu.VMEM((nd, LANES), jnp.float32),
-        ],
-        compiler_params=pltpu.CompilerParams(vmem_limit_bytes=40 * 1024 * 1024),
-        name="finish_step",
-    )(dia_offsets, dia_coef, wind_speed.reshape(1, npts), wind_dir.reshape(1, npts), blocks)
-    done = done.reshape(nd, NFREQ, 2, npts).transpose(0, 2, 1, 3)
+    done = finish_call(
+        nd * dirs, nd, nf, dia_offsets, dia_coef,
+        wind_speed.reshape(1, npts), wind_dir.reshape(1, npts), blocks,
+    )
+    done = done[:, :, : 2 * npts].reshape(nd, NFREQ, 2, npts).transpose(0, 2, 1, 3)
     return done.reshape(2 * nd, NFREQ, npts)
 
 

time: 63.8 us -> 57.3 us (0.90)
  Pallas kernels: 24.8 us -> 21.1 us
  blocking collectives: 36.9 us -> 34.2 us
    pallas_call x1, Pallas kernels: 6.25 us -> 3.27 us  [finish_call(): pl.pallas_call(functools.partial(finish_kernel, ndirs), out_shape=jax.Sha...]
    all_to_all x1, blocking collectives: 36.9 us -> 34.2 us  [on_device(): lax.all_to_all(blocks, ('dir', 'freq'), split_axis=0, concat_axis=0, tile...]
    pallas_call x1, Pallas kernels: 18.5 us -> 17.8 us  [local_call(): pl.pallas_call(functools.partial(local_scoped, ndirs), out_shape=jax.Shap...]
where the time goes in v3:
time: 57.3 us; the launch traced here: 57.2 us
  blocking collectives  34.2 us (60%)
  Pallas kernels  21.1 us (37%)
  local copies, waits for them, and re-layouts  1.78 us (3%)
    all_to_all x1, blocking collectives, on_device(): lax.all_to_all(blocks, ('dir', 'freq'), split_axis=0, concat_axis=0, tile...  34.2 us
    pallas_call x1, Pallas kernels, local_call(): pl.pallas_call(functools.partial(local_scoped, ndirs), out_shape=jax.Shap...  17.8 us
    pallas_call x1, Pallas kernels, finish_call(): pl.pallas_call(functools.partial(finish_kernel, ndirs), out_shape=jax.Sha...  3.27 us
    reshape x1, local copies, waits for them, and re-layouts, on_device(): return done.reshape(2 * nd, NFREQ, npts)  1.49 us

profile of v3, /device:TPU:1, one launch (start us, length us, event | category | flops | bytes accessed | tf_op | source)
XLA Modules:
  0.0 57.2 jit_solution(11318451005071266435)
XLA Ops:
  0.0 0.0 copy-start.3
  0.0 0.0 copy-start.2
  0.0 0.0 copy-start.1
  0.0 0.0 copy-start
  0.0 17.8 %local_step.1 = bf16[768,2,128]{2,1,0:T(2,128)(2,1)S(1)} custom-call(f32[6,2,8192]{2,1,0:T(2,128)} %bitcast.9, s32[6,8192]{1,0:T(8,128)} %refs_1_.1, f32[6,8192]{1,0:T(8,128)} %refs_2_.1, f32[6,8192]{1,0:T(8,128)} %refs_3_.1, s32[1,8192]{1,0:T(1,128)} %bitcast.10, s32[1,8192]{1,0:T(1,128)} %bitcast.11), custom_call_target="tpu_custom_call" | custom-call | tf_op jit(solution)/shard_map/local_step/pallas_call | solution.py:352
  17.8 34.2 %all_to_all.5.blocks = bf16[768,2,128]{2,1,0:T(2,128)(2,1)S(1)} all-to-all(bf16[768,2,128]{2,1,0:T(2,128)(2,1)S(1)} %local_step.1), channel_id=1, replica_groups=mesh['dir'=32,'freq'=8] {'dir','freq'}, dimensions={0} | all-to-all | bytes 786432 | tf_op jit(solution)/shard_map/all_to_all | solution.py:427
  52.0 0.0 copy-done.3
  52.0 0.0 copy-done.2
  52.0 0.0 copy-done.1
  52.0 0.0 copy-done
  52.0 3.3 %finish_step.1 = f32[32,48,128]{2,1,0:T(8,128)S(1)} custom-call(s32[2,3]{1,0:T(2,128)S(1)} %copy-done, f32[3]{0:T(128)S(1)} %copy-done.1, f32[1,32]{1,0:T(1,128)S(1)} %bitcast.6, f32[1,32]{1,0:T(1,128)S(1)} %bitcast.7, bf16[768,2,128]{2,1,0:T(2,128)(2,1)S(1)} %all_to_all.5.blocks), custom_call_target="tpu_custom_call" | custom-call | tf_op jit(solution)/shard_map/finish_step/pallas_call | solution.py:393
  55.3 0.3 fusion
  55.5 0.2 pad_maximum_fusion
  55.7 1.5 %copy.19 = f32[64,48,32]{0,2,1:T(8,128)} copy(f32[64,48,32]{2,1,0:T(8,128)S(1)} %bitcast.8) | data formatting | bytes 786432 | tf_op jit(solution)/shard_map/reshape | solution.py:434
Async XLA Ops:
  0.0 52.0 %copy-start.3 = (f32[32]{0:T(128)S(1)}, f32[32]{0:T(128)}, u32[]{:S(2)}) copy-start(f32[32]{0:T(128)} %param.19) | copy-start | bytes 388
  0.0 52.0 %copy-start.2 = (f32[32]{0:T(128)S(1)}, f32[32]{0:T(128)}, u32[]{:S(2)}) copy-start(f32[32]{0:T(128)} %param.18) | copy-start | bytes 388
  0.0 52.0 %copy-start.1 = (f32[3]{0:T(128)S(1)}, f32[3]{0:T(128)}, u32[]{:S(2)}) copy-start(f32[3]{0:T(128)} %strength.1) | copy-start | bytes 40
  0.0 52.0 %copy-start = (s32[2,3]{1,0:T(2,128)S(1)}, s32[2,3]{1,0:T(2,128)}, u32[]{:S(2)}) copy-start(s32[2,3]{1,0:T(2,128)} %offsets.1) | copy-start | bytes 76

commit v4 on v3

--- a/solution.py
+++ b/solution.py
@@ -22,13 +22,26 @@
 
 LANES = 128
 TILE = 256
-WIDEN, UNPACK, TRANSFER, GROW = 8, 8, 4, 8
-STAGE, ADVECT, SWAP = 2, 8, 8
+WIDEN, UNPACK, TRANSFER, GROW, PLACE = 8, 8, 4, 8, 4
+STAGE, ADVECT, SWAP = 4, 8, 16
+ROUND = 1.5 * 2.0**23
+SINE = (1.0, -0.16666667, 0.008333329, -0.00019840701, 2.7518759e-06, -2.3793149e-08)
 CENTRE = 0.5
 
 
 def sigma_of(index):
     return SIG_LO * jnp.exp(index.astype(jnp.float32) * (math.log(SIG_HI / SIG_LO) / (NFREQ - 1)))
+
+
+def cosine(x):
+    turns = (x * (0.5 / math.pi) + ROUND) - ROUND
+    h = (x * 0.5 - turns * 3.140625) - turns * (math.pi - 3.140625)
+    z = h * h
+    p = SINE[-1]
+    for c in SINE[-2::-1]:
+        p = p * z + c
+    s = p * h
+    return 1.0 - 2.0 * (s * s)
 
 
 def one_hot(low, ramp):
@@ -120,7 +133,7 @@
                 geom = []
                 for i in range(dirs):
                     theta = (2.0 * math.pi / ndirs) * (first_dir + i).astype(jnp.float32)
-                    bearing = jnp.cos(theta - angle[:, at])
+                    bearing = cosine(theta - angle[:, at])
                     geom.append(coef[:, at] * jnp.maximum(bearing, 0.0))
             high = highs.pop(n)
             match = [high == sub + 8 * h for h in range(groups)]
@@ -213,7 +226,7 @@
 
 
 def finish_kernel(
-    ndirs, offsets, strength, wind_speed, wind_dir, blocks, out, table, relaid, rows, lines
+    ndirs, offsets, strength, wind_speed, wind_dir, blocks, out_at, table, relaid, rows, lines, turned, out, left
 ):
     pairs = ndirs // 2
     reach = DSPAN // 2
@@ -318,18 +331,37 @@
     step = lax.broadcasted_iota(jnp.int32, (pairs, LANES), 0) * 2 + jnp.bitwise_and(
         jnp.right_shift(lax.broadcasted_iota(jnp.int32, (pairs, LANES), 1), 5), 1
     )
-    rows[...] = jnp.cos((2.0 * math.pi / ndirs) * step.astype(jnp.float32) - towards)
+    rows[...] = cosine((2.0 * math.pi / ndirs) * step.astype(jnp.float32) - towards)
 
     def grow(s, carry):
         along = rows[pl.ds(s, 1), :]
         for b in range(lots):
             growth = push[b] * jnp.maximum(wind[b] * along - 1.0, 0.0)
             value = relaid[b, s] * (1.0 + growth) * damp[b]
-            out[s, pl.ds(2 * b, 8, stride=2 * lots), :] = value
-            out[s, pl.ds(2 * b + 1, 8, stride=2 * lots), :] = pltpu.roll(value, 64, 1)
-        return carry
-
+            quarter = pltpu.roll(value, LANES - 32, 1)
+            even = jnp.where(low, value, quarter)
+            odd = jnp.where(low, quarter, pltpu.roll(value, 64, 1))
+            for i, part in enumerate((even, odd)):
+                turned[pl.ds(b * ndirs + 2 * s + i, 8, stride=lots * ndirs), :] = part
+        return carry
+
+    low = lane < 32
     lax.fori_loop(0, pairs, grow, 0, unroll=GROW)
+
+    def place(a, carry):
+        for b in range(lots):
+            spot = pl.ds(pl.multiple_of((a * lots + b) * ndirs, ndirs), ndirs)
+            flat = jnp.swapaxes(turned[spot, :], 0, 1)
+            for x in range(2):
+                out[a * 2 * lots + 2 * b + x] = flat[32 * x : 32 * x + 32]
+        spot = pl.ds(a * 2 * lots, 2 * lots)
+        pltpu.make_async_copy(out.at[spot], out_at.at[spot], left.at[a]).start()
+        return carry
+
+    lax.fori_loop(0, 8, place, 0, unroll=PLACE)
+    for a in range(8):
+        spot = pl.ds(a * 2 * lots, 2 * lots)
+        pltpu.make_async_copy(out.at[spot], out_at.at[spot], left.at[a]).wait()
 
 
 def local_scoped(ndirs, *refs):
@@ -392,14 +424,17 @@
     lots = blocks.shape[0] // (nd * nf)
     return pl.pallas_call(
         functools.partial(finish_kernel, ndirs),
-        out_shape=jax.ShapeDtypeStruct((nd, NFREQ, LANES), jnp.float32),
+        out_shape=jax.ShapeDtypeStruct((NFREQ, LANES // 4, ndirs), jnp.float32),
         in_specs=[smem, smem, vmem, vmem, vmem],
-        out_specs=vmem,
+        out_specs=pl.BlockSpec(memory_space=pltpu.MemorySpace.HBM),
         scratch_shapes=[
             pltpu.VMEM((2, 2, lots + 2, nd + DSPAN, nf, LANES), jnp.float32),
             pltpu.VMEM((lots, nd, nf, LANES), jnp.float32),
             pltpu.VMEM((nd, LANES), jnp.float32),
             pltpu.VMEM((2 * nf * lots * nd, LANES), jnp.float32),
+            pltpu.VMEM((nf * lots * ndirs, LANES), jnp.float32),
+            pltpu.VMEM((NFREQ, LANES // 4, ndirs), jnp.float32),
+            pltpu.SemaphoreType.DMA((nf,)),
         ],
         compiler_params=pltpu.CompilerParams(vmem_limit_bytes=40 * 1024 * 1024),
         name="finish_step",
@@ -430,8 +465,7 @@
         nd * dirs, nd, nf, dia_offsets, dia_coef,
         wind_speed.reshape(1, npts), wind_dir.reshape(1, npts), blocks,
     )
-    done = done[:, :, : 2 * npts].reshape(nd, NFREQ, 2, npts).transpose(0, 2, 1, 3)
-    return done.reshape(2 * nd, NFREQ, npts)
+    return done.transpose(2, 0, 1)
 
 
 def solution(mesh):

time: 57.3 us -> 56.5 us (0.986)
  local copies, waits for them, and re-layouts: 1.78 us -> 0.68 us
    pallas_call x1, Pallas kernels: 3.27 us -> 4.81 us  [finish_call(): pl.pallas_call(functools.partial(finish_kernel, ndirs), out_shape=jax.Sha...]
    reshape x1 -> x0, local copies, waits for them, and re-layouts: 1.49 us -> none  [on_device(): return done.reshape(2 * nd, NFREQ, npts)]
    pallas_call x1, Pallas kernels: 17.8 us -> 16.8 us  [local_call(): pl.pallas_call(functools.partial(local_scoped, ndirs), out_shape=jax.Shap...]
    unnamed x8, local copies, waits for them, and re-layouts: 0.02 us -> 0.68 us
where the time goes in v4:
time: 56.5 us; the launch traced here: 56.4 us
  blocking collectives  34.2 us (61%)
  Pallas kernels  21.6 us (38%)
  local copies, waits for them, and re-layouts  0.68 us (1%)
    all_to_all x1, blocking collectives, on_device(): lax.all_to_all(blocks, ('dir', 'freq'), split_axis=0, concat_axis=0, tile...  34.2 us
    pallas_call x1, Pallas kernels, local_call(): pl.pallas_call(functools.partial(local_scoped, ndirs), out_shape=jax.Shap...  16.8 us
    pallas_call x1, Pallas kernels, finish_call(): pl.pallas_call(functools.partial(finish_kernel, ndirs), out_shape=jax.Sha...  4.81 us

profile of v4, /device:TPU:1, one launch (start us, length us, event | category | flops | bytes accessed | tf_op | source)
XLA Modules:
  0.0 56.4 jit_solution(2485517463557451128)
XLA Ops:
  0.0 16.8 %local_step.1 = bf16[768,2,128]{2,1,0:T(2,128)(2,1)S(1)} custom-call(f32[6,2,8192]{2,1,0:T(2,128)} %bitcast.8, s32[6,8192]{1,0:T(8,128)} %refs_1_.1, f32[6,8192]{1,0:T(8,128)} %refs_2_.1, f32[6,8192]{1,0:T(8,128)} %refs_3_.1, s32[1,8192]{1,0:T(1,128)} %bitcast.9, s32[1,8192]{1,0:T(1,128)} %bitcast.10), custom_call_target="tpu_custom_call" | custom-call | tf_op jit(solution)/shard_map/local_step/pallas_call | solution.py:384
  16.8 0.0 copy-start.2
  16.8 0.0 copy-start.3
  16.8 34.2 %all_to_all.5.blocks = bf16[768,2,128]{2,1,0:T(2,128)(2,1)S(1)} all-to-all(bf16[768,2,128]{2,1,0:T(2,128)(2,1)S(1)} %local_step.1), channel_id=1, replica_groups=mesh['dir'=32,'freq'=8] {'dir','freq'}, dimensions={0} | all-to-all | bytes 786432 | tf_op jit(solution)/shard_map/all_to_all | solution.py:462
  51.0 0.0 copy-start
  51.0 0.0 copy-start.1
  51.0 0.0 copy-done.2
  51.0 0.0 copy-done.3
  51.0 0.7 %copy-done = s32[2,3]{1,0:T(2,128)S(1)} copy-done((s32[2,3]{1,0:T(2,128)S(1)}, s32[2,3]{1,0:T(2,128)}, u32[]{:S(2)}) %copy-start) | copy-done | bytes 48
  51.6 0.0 copy-done.1
  51.6 4.8 %finish_step.1 = f32[48,32,64]{2,1,0:T(8,128)} custom-call(s32[2,3]{1,0:T(2,128)S(1)} %copy-done, f32[3]{0:T(128)S(1)} %copy-done.1, f32[1,32]{1,0:T(1,128)S(1)} %bitcast.6, f32[1,32]{1,0:T(1,128)S(1)} %bitcast.7, bf16[768,2,128]{2,1,0:T(2,128)(2,1)S(1)} %all_to_all.5.blocks), custom_call_target="tpu_custom_call" | custom-call | tf_op jit(solution)/shard_map/finish_step/pallas_call | solution.py:425
Async XLA Ops:
  16.8 34.2 %copy-start.2 = (f32[32]{0:T(128)S(1)}, f32[32]{0:T(128)}, u32[]{:S(2)}) copy-start(f32[32]{0:T(128)} %param.18) | copy-start | bytes 388
  16.8 34.2 %copy-start.3 = (f32[32]{0:T(128)S(1)}, f32[32]{0:T(128)}, u32[]{:S(2)}) copy-start(f32[32]{0:T(128)} %param.19) | copy-start | bytes 388
  51.0 0.7 %copy-start = (s32[2,3]{1,0:T(2,128)S(1)}, s32[2,3]{1,0:T(2,128)}, u32[]{:S(2)}) copy-start(s32[2,3]{1,0:T(2,128)} %offsets.1) | copy-start | bytes 76
  51.0 0.7 %copy-start.1 = (f32[3]{0:T(128)S(1)}, f32[3]{0:T(128)}, u32[]{:S(2)}) copy-start(f32[3]{0:T(128)} %strength.1) | copy-start | bytes 40

commit v5 on v4

--- a/solution.py
+++ b/solution.py
@@ -22,8 +22,8 @@
 
 LANES = 128
 TILE = 256
-WIDEN, UNPACK, TRANSFER, GROW, PLACE = 8, 8, 4, 8, 4
-STAGE, ADVECT, SWAP = 4, 8, 16
+WIDEN, UNPACK, TRANSFER, GROW, PLACE = 8, 8, 8, 16, 4
+STAGE, ADVECT, SWAP = 4, 16, 32
 ROUND = 1.5 * 2.0**23
 SINE = (1.0, -0.16666667, 0.008333329, -0.00019840701, 2.7518759e-06, -2.3793149e-08)
 CENTRE = 0.5
@@ -226,8 +226,16 @@
 
 
 def finish_kernel(
-    ndirs, offsets, strength, wind_speed, wind_dir, blocks, out_at, table, relaid, rows, lines, turned, out, left
+    ndirs, offsets_at, strength_at, speed_at, dir_at, blocks, out_at,
+    offsets, strength, wind_speed, wind_dir, arrived, table, relaid, rows, lines, turned, out, left
 ):
+    small = [(offsets_at, offsets), (strength_at, strength)]
+    small += [(speed_at, wind_speed), (dir_at, wind_dir)]
+    copies = [
+        pltpu.make_async_copy(src, dst, arrived.at[n]) for n, (src, dst) in enumerate(small)
+    ]
+    for copy in copies:
+        copy.start()
     pairs = ndirs // 2
     reach = DSPAN // 2
     lots = table.shape[2] - 2
@@ -274,6 +282,8 @@
                     table[i, j, b, s] = table[i, j, b, s + pairs]
                     table[i, j, b, s + pairs + reach] = table[i, j, b, s + reach]
 
+    for copy in copies:
+        copy.wait()
     shapes = []
     for q in range(strength.shape[0]):
         d, m, c = offsets[0, q], offsets[1, q], strength[q]
@@ -420,14 +430,19 @@
 
 def finish_call(ndirs, nd, nf, dia_offsets, dia_coef, wind_speed, wind_dir, blocks):
     vmem = pl.BlockSpec(memory_space=pltpu.VMEM)
-    smem = pl.BlockSpec(memory_space=pltpu.SMEM)
+    hbm = pl.BlockSpec(memory_space=pltpu.MemorySpace.HBM)
     lots = blocks.shape[0] // (nd * nf)
     return pl.pallas_call(
         functools.partial(finish_kernel, ndirs),
         out_shape=jax.ShapeDtypeStruct((NFREQ, LANES // 4, ndirs), jnp.float32),
-        in_specs=[smem, smem, vmem, vmem, vmem],
+        in_specs=[hbm, hbm, hbm, hbm, vmem],
         out_specs=pl.BlockSpec(memory_space=pltpu.MemorySpace.HBM),
         scratch_shapes=[
+            pltpu.SMEM(dia_offsets.shape, jnp.int32),
+            pltpu.SMEM(dia_coef.shape, jnp.float32),
+            pltpu.VMEM(wind_speed.shape, jnp.float32),
+            pltpu.VMEM(wind_dir.shape, jnp.float32),
+            pltpu.SemaphoreType.DMA((4,)),
             pltpu.VMEM((2, 2, lots + 2, nd + DSPAN, nf, LANES), jnp.float32),
             pltpu.VMEM((lots, nd, nf, LANES), jnp.float32),
             pltpu.VMEM((nd, LANES), jnp.float32),
@@ -438,7 +453,13 @@
         ],
         compiler_params=pltpu.CompilerParams(vmem_limit_bytes=40 * 1024 * 1024),
         name="finish_step",
-    )(dia_offsets, dia_coef, wind_speed, wind_dir, blocks)
+    )(
+        *(
+            pltpu.with_memory_space_constraint(x, pltpu.MemorySpace.HBM)
+            for x in (dia_offsets, dia_coef, wind_speed, wind_dir)
+        ),
+        blocks,
+    )
 
 
 def on_device(

time: 56.5 us -> 54.4 us (0.963)
  Pallas kernels: 21.6 us -> 20.1 us
  local copies, waits for them, and re-layouts: 0.68 us -> 0 us
    pallas_call x1, Pallas kernels: 4.81 us -> 4.06 us  [finish_call(): pl.pallas_call(functools.partial(finish_kernel, ndirs), out_shape=jax.Sha...]
    pallas_call x1, Pallas kernels: 16.8 us -> 16 us  [local_call(): pl.pallas_call(functools.partial(local_scoped, ndirs), out_shape=jax.Shap...]
    unnamed x8 -> x0, local copies, waits for them, and re-layouts: 0.68 us -> none
where the time goes in v5:
time: 54.4 us; the launch traced here: 54.3 us
  blocking collectives  34.2 us (63%)
  Pallas kernels  20.1 us (37%)
    all_to_all x1, blocking collectives, on_device(): lax.all_to_all(blocks, ('dir', 'freq'), split_axis=0, concat_axis=0, tile...  34.2 us
    pallas_call x1, Pallas kernels, local_call(): pl.pallas_call(functools.partial(local_scoped, ndirs), out_shape=jax.Shap...  16 us
    pallas_call x1, Pallas kernels, finish_call(): pl.pallas_call(functools.partial(finish_kernel, ndirs), out_shape=jax.Sha...  4.06 us

profile of v5, /device:TPU:1, one launch (start us, length us, event | category | flops | bytes accessed | tf_op | source)
XLA Modules:
  0.0 54.3 jit_solution(14430091632288510216)
XLA Ops:
  0.0 16.0 %local_step.1 = bf16[768,2,128]{2,1,0:T(2,128)(2,1)S(1)} custom-call(f32[6,2,8192]{2,1,0:T(2,128)} %bitcast.6, s32[6,8192]{1,0:T(8,128)} %refs_1_.1, f32[6,8192]{1,0:T(8,128)} %refs_2_.1, f32[6,8192]{1,0:T(8,128)} %refs_3_.1, s32[1,8192]{1,0:T(1,128)} %bitcast.7, s32[1,8192]{1,0:T(1,128)} %bitcast.8), custom_call_target="tpu_custom_call" | custom-call | tf_op jit(solution)/shard_map/local_step/pallas_call | solution.py:394
  16.1 34.2 %all_to_all.5.blocks = bf16[768,2,128]{2,1,0:T(2,128)(2,1)S(1)} all-to-all(bf16[768,2,128]{2,1,0:T(2,128)(2,1)S(1)} %local_step.1), channel_id=1, replica_groups=mesh['dir'=32,'freq'=8] {'dir','freq'}, dimensions={0} | all-to-all | bytes 786432 | tf_op jit(solution)/shard_map/all_to_all | solution.py:483
  50.2 4.1 %finish_step.1 = f32[48,32,64]{2,1,0:T(8,128)} custom-call(s32[2,3]{1,0:T(2,128)} %offsets_at.1, f32[3]{0:T(128)} %strength_at.1, f32[1,32]{1,0:T(1,128)} %bitcast.9, f32[1,32]{1,0:T(1,128)} %bitcast.10, bf16[768,2,128]{2,1,0:T(2,128)(2,1)S(1)} %all_to_all.5.blocks), custom_call_target="tpu_custom_call" | custom-call | tf_op jit(solution)/shard_map/finish_step/pallas_call | solution.py:435

commit v6 on v5

--- a/solution.py
+++ b/solution.py
@@ -91,7 +91,7 @@
 
     lax.fori_loop(0, tiles, stage, 0, unroll=STAGE)
     for c in range(TILE // LANES):
-        pick[:, c * LANES : (c + 1) * LANES] = pickf[c].astype(jnp.bfloat16)
+        pick[:, c * LANES : (c + 1) * LANES] = pickf[c, : pick.shape[0]].astype(jnp.bfloat16)
     for copy in copies[2:5]:
         copy.wait()
 
@@ -169,7 +169,7 @@
 
     lax.fori_loop(0, tiles // ADVECT, advect, 0)
     for c in range(TILE // LANES):
-        keep[:, c * LANES : (c + 1) * LANES] = keepf[c].astype(jnp.bfloat16)
+        keep[:, c * LANES : (c + 1) * LANES] = keepf[c, : keep.shape[0]].astype(jnp.bfloat16)
     copies[5].wait()
 
     row = sub[:, :LANES]
@@ -405,9 +405,9 @@
             pltpu.VMEM((1, npoints), jnp.int32),
             pltpu.SemaphoreType.DMA((6,)),
             pltpu.VMEM((dirs, 8, npoints), jnp.float32),
-            pltpu.VMEM((TILE // LANES, dirs * freqs * tiles, LANES), jnp.float32),
+            pltpu.VMEM((TILE // LANES, (dirs * freqs + 2) * tiles, LANES), jnp.float32),
             pltpu.VMEM((dirs * freqs * tiles, TILE), jnp.bfloat16),
-            pltpu.VMEM((TILE // LANES, 2 * dirs * freqs * tiles, LANES), jnp.float32),
+            pltpu.VMEM((TILE // LANES, 2 * dirs * freqs * tiles + 8, LANES), jnp.float32),
             pltpu.VMEM((2 * dirs * freqs * tiles, TILE), jnp.bfloat16),
             pltpu.VMEM((TILE, TILE), jnp.bfloat16),
         ],

time: 54.4 us -> 54.4 us (level)
  no operation moved by 1% of the time
where the time goes in v6:
time: 54.4 us; the launch traced here: 54.3 us
  blocking collectives  34.2 us (63%)
  Pallas kernels  20.1 us (37%)
    all_to_all x1, blocking collectives, on_device(): lax.all_to_all(blocks, ('dir', 'freq'), split_axis=0, concat_axis=0, tile...  34.2 us
    pallas_call x1, Pallas kernels, local_call(): pl.pallas_call(functools.partial(local_scoped, ndirs), out_shape=jax.Shap...  16 us
    pallas_call x1, Pallas kernels, finish_call(): pl.pallas_call(functools.partial(finish_kernel, ndirs), out_shape=jax.Sha...  4.1 us

profile of v6, /device:TPU:1, one launch (start us, length us, event | category | flops | bytes accessed | tf_op | source)
XLA Modules:
  0.0 54.3 jit_solution(7298327236478775277)
XLA Ops:
  0.0 16.0 %local_step.1 = bf16[768,2,128]{2,1,0:T(2,128)(2,1)S(1)} custom-call(f32[6,2,8192]{2,1,0:T(2,128)} %bitcast.6, s32[6,8192]{1,0:T(8,128)} %refs_1_.1, f32[6,8192]{1,0:T(8,128)} %refs_2_.1, f32[6,8192]{1,0:T(8,128)} %refs_3_.1, s32[1,8192]{1,0:T(1,128)} %bitcast.7, s32[1,8192]{1,0:T(1,128)} %bitcast.8), custom_call_target="tpu_custom_call" | custom-call | tf_op jit(solution)/shard_map/local_step/pallas_call | solution.py:394
  16.0 34.2 %all_to_all.5.blocks = bf16[768,2,128]{2,1,0:T(2,128)(2,1)S(1)} all-to-all(bf16[768,2,128]{2,1,0:T(2,128)(2,1)S(1)} %local_step.1), channel_id=1, replica_groups=mesh['dir'=32,'freq'=8] {'dir','freq'}, dimensions={0} | all-to-all | bytes 786432 | tf_op jit(solution)/shard_map/all_to_all | solution.py:483
  50.2 4.1 %finish_step.1 = f32[48,32,64]{2,1,0:T(8,128)} custom-call(s32[2,3]{1,0:T(2,128)} %offsets_at.1, f32[3]{0:T(128)} %strength_at.1, f32[1,32]{1,0:T(1,128)} %bitcast.9, f32[1,32]{1,0:T(1,128)} %bitcast.10, bf16[768,2,128]{2,1,0:T(2,128)(2,1)S(1)} %all_to_all.5.blocks), custom_call_target="tpu_custom_call" | custom-call | tf_op jit(solution)/shard_map/finish_step/pallas_call | solution.py:435

commit v7 on v6

--- a/solution.py
+++ b/solution.py
@@ -22,8 +22,8 @@
 
 LANES = 128
 TILE = 256
-WIDEN, UNPACK, TRANSFER, GROW, PLACE = 8, 8, 8, 16, 4
-STAGE, ADVECT, SWAP = 4, 16, 32
+WIDEN, UNPACK, TRANSFER, GROW, PLACE = 8, 8, 16, 16, 8
+STAGE, ADVECT, SWAP = 4, 32, 32
 ROUND = 1.5 * 2.0**23
 SINE = (1.0, -0.16666667, 0.008333329, -0.00019840701, 2.7518759e-06, -2.3793149e-08)
 CENTRE = 0.5

time: 54.4 us -> 54.4 us (level)
  no operation moved by 1% of the time
where the time goes in v7:
time: 54.4 us; the launch traced here: 54.3 us
  blocking collectives  34.2 us (63%)
  Pallas kernels  20 us (37%)
    all_to_all x1, blocking collectives, on_device(): lax.all_to_all(blocks, ('dir', 'freq'), split_axis=0, concat_axis=0, tile...  34.2 us
    pallas_call x1, Pallas kernels, local_call(): pl.pallas_call(functools.partial(local_scoped, ndirs), out_shape=jax.Shap...  15.9 us
    pallas_call x1, Pallas kernels, finish_call(): pl.pallas_call(functools.partial(finish_kernel, ndirs), out_shape=jax.Sha...  4.06 us

profile of v7, /device:TPU:1, one launch (start us, length us, event | category | flops | bytes accessed | tf_op | source)
XLA Modules:
  0.0 54.3 jit_solution(779787945495045514)
XLA Ops:
  0.0 15.9 %local_step.1 = bf16[768,2,128]{2,1,0:T(2,128)(2,1)S(1)} custom-call(f32[6,2,8192]{2,1,0:T(2,128)} %bitcast.6, s32[6,8192]{1,0:T(8,128)} %refs_1_.1, f32[6,8192]{1,0:T(8,128)} %refs_2_.1, f32[6,8192]{1,0:T(8,128)} %refs_3_.1, s32[1,8192]{1,0:T(1,128)} %bitcast.7, s32[1,8192]{1,0:T(1,128)} %bitcast.8), custom_call_target="tpu_custom_call" | custom-call | tf_op jit(solution)/shard_map/local_step/pallas_call | solution.py:394
  15.9 34.2 %all_to_all.5.blocks = bf16[768,2,128]{2,1,0:T(2,128)(2,1)S(1)} all-to-all(bf16[768,2,128]{2,1,0:T(2,128)(2,1)S(1)} %local_step.1), channel_id=1, replica_groups=mesh['dir'=32,'freq'=8] {'dir','freq'}, dimensions={0} | all-to-all | bytes 786432 | tf_op jit(solution)/shard_map/all_to_all | solution.py:483
  50.1 4.1 %finish_step.1 = f32[48,32,64]{2,1,0:T(8,128)} custom-call(s32[2,3]{1,0:T(2,128)} %offsets_at.1, f32[3]{0:T(128)} %strength_at.1, f32[1,32]{1,0:T(1,128)} %bitcast.9, f32[1,32]{1,0:T(1,128)} %bitcast.10, bf16[768,2,128]{2,1,0:T(2,128)(2,1)S(1)} %all_to_all.5.blocks), custom_call_target="tpu_custom_call" | custom-call | tf_op jit(solution)/shard_map/finish_step/pallas_call | solution.py:435
